TPU v7x, 32 devices: a whole 2x2x4 slice. The times are simulated.
32 devices in a mesh: batch: 8 (over y, x, core), seq: 4 (over z).
Axes of the slice: x: 2, y: 2, z: 4, core: 2. Of those that a mesh axis runs over, the one named last changes fastest.
Arguments:
- activations: float32 [8, 512, 960], P('batch', 'seq'), may hold values from -8 to 8
- segment_ids: int32 [8, 512], P('batch', 'seq'), may hold values from 0 to 2, never falling along the last dimension, each value on 1 to 384 neighbouring positions
- attention_gain: float32 [960], replicated, may hold values from 0.5 to 1.5
- query_weight: bfloat16 [960, 960], P('batch', 'seq'), may hold values from -0.117657917 to 0.117657917
- key_weight: bfloat16 [960, 320], P('batch', 'seq'), may hold values from -0.117657917 to 0.117657917
- value_weight: bfloat16 [960, 320], P('batch', 'seq'), may hold values from -0.1875 to 0.1875
- output_weight: bfloat16 [960, 960], P('batch', 'seq'), may hold values from -0.75 to 0.75
- feed_gain: float32 [960], replicated, may hold values from 0.5 to 1.5
- gate_weight: bfloat16 [960, 2560], P('batch', 'seq'), may hold values from -0.1875 to 0.1875
- up_weight: bfloat16 [960, 2560], P('batch', 'seq'), may hold values from -0.1875 to 0.1875
- down_weight: bfloat16 [2560, 960], P('seq', 'batch'), may hold values from -0.125 to 0.125
- out_grad: float32 [8, 512, 960], P('batch', 'seq'), may hold values from -6 to 6
Outputs:
- block_output: float32 [8, 512, 960], P('batch', 'seq')
- input_grad: float32 [8, 512, 960], P('batch', 'seq')
- attention_gain_grad: float32 [960], replicated
- query_weight_grad: float32 [960, 960], P('batch', 'seq')
- key_weight_grad: float32 [960, 320], P('batch', 'seq')
- value_weight_grad: float32 [960, 320], P('batch', 'seq')
- output_weight_grad: float32 [960, 960], P('batch', 'seq')
- feed_gain_grad: float32 [960], replicated
- gate_weight_grad: float32 [960, 2560], P('batch', 'seq')
- up_weight_grad: float32 [960, 2560], P('batch', 'seq')
- down_weight_grad: float32 [2560, 960], P('seq', 'batch')
All inputs are finite; a program needn't handle non-finite values.
Results may differ from a plain program's by a relative error of at most 0.014.
The roundings to bfloat16 on the way count: a program that leaves them out, or rounds other values in their place, can miss the bound.
Values may be sent and summed in bfloat16 or wider, within the bound.
No kernel may reach another device: no remote copies, remote signals or barrier semaphores. Data moves between devices by JAX's collectives and lax.ppermute only.
A program may use at most 128 MiB of HBM per device.

v0:
```python
import functools
import math

import jax
import jax.numpy as jnp
from jax import lax
from jax.experimental import pallas as pl
from jax.experimental.pallas import tpu as pltpu
from jax.sharding import PartitionSpec as P


HEADS = 15
KV_HEADS = 5
HEAD_DIM = 64
GROUPS = HEADS // KV_HEADS
KV_WIDTH = KV_HEADS * HEAD_DIM
HALF = HEAD_DIM // 2
INV_ROOT = 1.0 / HEAD_DIM**0.5
BF = jnp.bfloat16
F32 = jnp.float32
ROOM = 6


def rotary_tables(positions):
    expon = jnp.arange(HALF, dtype=F32) * (2.0 / HEAD_DIM)
    inverse = jnp.power(F32(10000.0), -expon)
    angles = positions[:, None] * inverse[None, :]
    return jnp.cos(angles), jnp.sin(angles)


def mmul(left, right):
    return jnp.dot(left, right, preferred_element_type=F32)


def left_mmul(left, right):
    return lax.dot_general(left, right, (((0,), (0,)), ((), ())), preferred_element_type=F32)


def right_mmul(left, right):
    return lax.dot_general(left, right, (((1,), (1,)), ((), ())), preferred_element_type=F32)


def head_of(h):
    return slice(h * HEAD_DIM, (h + 1) * HEAD_DIM)


def tables(cosine, sine):
    c, d = cosine[...], sine[...]
    return jnp.concatenate([c, c], 1), jnp.concatenate([-d, d], 1)


def swapped(x):
    return jnp.concatenate([x[:, HALF:], x[:, :HALF]], 1)


def rms_scale(rows):
    return lax.rsqrt(jnp.mean(rows * rows, -1, keepdims=True) + 1e-05)


def norm_back(grad_out, normed, scale, gain):
    scaled = grad_out * gain
    inner = jnp.mean(scaled * normed, -1, keepdims=True)
    return (scale * (scaled - normed * inner), jnp.sum(grad_out * normed, 0, keepdims=True))


def split_lanes(ref, value, count):
    wide = value.shape[1] // count
    for j in range(count):
        ref[j] = value[:, j * wide : (j + 1) * wide]


def join_lanes(ref, count):
    return jnp.concatenate([ref[j] for j in range(count)], 1)


def blocks(near, far):
    b = lax.axis_index("batch")
    out = []
    for core, refs in ((0, near), (1, far)):
        for m, ref in enumerate(refs):
            out.append((ref, core, m, b ^ (2 * m + core)))
    return out


def take(refs, *counts):
    out = []
    at = 0
    for n in counts:
        out.append(refs[at] if n is None else refs[at : at + n])
        at += 1 if n is None else n
    assert at == len(refs)
    return out


def kv_kernel(chips, *refs):
    rows, gain, cosine, sine, seg, near, far, hidden, packet, hid3, acc4 = take(
        refs, *[None] * 5, chips, chips, *[None] * 4
    )
    line = near[0].shape[0]
    s = lax.axis_index("seq")
    piece = rows.shape[1]
    cos, sin = tables(cosine, sine)
    x = rows[...].T
    hid = (x * rms_scale(x) * gain[...]).astype(BF)
    hidden[...] = hid
    split_lanes(hid3, hid, hid3.shape[0])
    for k in range(line):
        acc = 0.0
        for ref, _, m, at in blocks(near, far):
            acc = acc + mmul(hid3[at], ref[k])
        acc4[s ^ k] = acc
    wide = near[0].shape[-1] // 2
    keys = jnp.concatenate([acc4[p, :, :wide] for p in range(line)], 1)
    values = jnp.concatenate([acc4[p, :, wide:] for p in range(line)], 1)
    for h in range(KV_HEADS):
        u = keys[:, head_of(h)]
        packet[:piece, head_of(h)] = (u * cos + swapped(u) * sin).astype(BF)
    packet[:piece, KV_WIDTH:] = values.astype(BF)
    packet[piece:, :] = jnp.zeros((packet.shape[0] - piece, packet.shape[1]), BF)
    packet[piece:, :piece] = jnp.broadcast_to(
        seg[...].astype(F32), (packet.shape[0] - piece, piece)
    ).astype(BF)


def query_kernel(chips, *refs):
    hidden, cosine, sine, near, far, query, hid3, acc4 = take(
        refs, None, None, None, chips, chips, None, None, None
    )
    line = near[0].shape[0]
    s = lax.axis_index("seq")
    cos, sin = tables(cosine, sine)
    split_lanes(hid3, hidden[...], hid3.shape[0])
    for k in range(line):
        acc = 0.0
        for ref, _, m, at in blocks(near, far):
            acc = acc + mmul(hid3[at], ref[k, 0])
        acc4[s ^ k] = acc
    full = join_lanes(acc4, line)
    for h in range(HEADS):
        u = full[:, head_of(h)]
        query[:, head_of(h)] = (u * cos + swapped(u) * sin).astype(BF)


def group_rows(ref, g):
    return jnp.concatenate([ref[:, head_of(GROUPS * g + i)] for i in range(GROUPS)], 0)


def slot_rows(packets, piece, lanes):
    return jnp.concatenate([p[:piece, lanes] for p in packets], 0)


def attention_kernel(chips, line, *refs):
    query, packets, rows, seg, gain, near, far, *rest = take(
        refs, None, line, None, None, None, chips, chips, *[None] * 7
    )
    probs, attn, mid, hidden, bias, att3, acc4 = rest
    s = lax.axis_index("seq")
    piece = rows.shape[1]
    mine = jnp.broadcast_to(seg[...].astype(F32), (piece, piece)).T
    at = lax.broadcasted_iota(jnp.int32, (piece, piece), 0)
    key = lax.broadcasted_iota(jnp.int32, (piece, piece), 1)
    for k in range(line):
        same = mine == packets[k][piece : piece + 1, :piece].astype(F32)
        ok = same & (key - k * piece <= at) & (key + (s - k) * piece >= 0)
        bias[:, k * piece : (k + 1) * piece] = jnp.where(ok, 0.0, -jnp.inf)
    for g in range(KV_HEADS):
        keys = slot_rows(packets, piece, head_of(g))
        values = slot_rows(packets, piece, head_of(KV_HEADS + g))
        scores = right_mmul(group_rows(query, g), keys) * INV_ROOT
        scores = scores + jnp.concatenate([bias[...]] * GROUPS, 0)
        raised = jnp.exp(scores - jnp.max(scores, -1, keepdims=True))
        weights = raised / jnp.sum(raised, -1, keepdims=True)
        probs[g] = weights
        out = mmul(weights.astype(BF), values).astype(BF)
        for i in range(GROUPS):
            attn[:, head_of(GROUPS * g + i)] = out[i * piece : (i + 1) * piece]
    split_lanes(att3, attn[...], att3.shape[0])
    for k in range(line):
        acc = 0.0
        for ref, _, m, j in blocks(near, far):
            acc = acc + mmul(att3[j], ref[k, 1])
        acc4[s ^ k] = acc
    x = rows[...].T + join_lanes(acc4, line)
    mid[...] = x
    hidden[...] = (x * rms_scale(x) * gain[...]).astype(BF)


def load_all(refs, scratch, sems):
    rows = refs[0].shape[0]
    copies = [
        pltpu.make_async_copy(ref, scratch.at[pl.ds(i * rows, rows)], sems.at[i])
        for i, ref in enumerate(refs)
    ]
    for copy in copies:
        copy.start()
    return copies


def load_slots(own, right, left, slots):
    s = lax.axis_index("seq")
    line = slots.shape[0]
    pltpu.sync_copy(own, slots.at[0])
    for k in range(1, line):
        for far in range(1, line):

            @pl.when((s ^ k) == s - far)
            def _():
                pltpu.sync_copy(right[far - 1], slots.at[k])

            @pl.when((s ^ k) == s + far)
            def _():
                pltpu.sync_copy(left[far - 1], slots.at[k])


def feed_kernel(chips, line, tile, *refs):
    hid, low, own, right, left, back_near, back_far, gate_s, up_s, inner_s, *scratch = take(
        refs, 2 * chips, 2 * chips, None, line - 1, line - 1, None, chips, *[None] * 12
    )
    slots, gate_w, up_w, down_w, hid_s, low_s, far_s, sems, far_sems = scratch
    copies = load_all(hid, hid_s, sems) + load_all(low, low_s, sems.at[pl.ds(2 * chips, 2 * chips)])
    load_slots(own, right, left, slots)
    piece = hid[0].shape[0]
    units = own.shape[0] // 3
    for k in range(line):
        span = slice(k * units, (k + 1) * units)
        gate_w[span] = slots[k, :units]
        up_w[span] = slots[k, units : 2 * units]
        down_w[span] = slots[k, 2 * units :]
    for copy in copies:
        copy.wait()
    half = chips * piece

    def run(back, base):
        def body(i, carry):
            span = pl.ds(pl.multiple_of(i * tile, tile), tile)
            read = pl.ds(pl.multiple_of(base + i * tile, tile), tile)
            h = hid_s[read]
            gate = right_mmul(h, gate_w[...])
            up = right_mmul(h, up_w[...])
            inner_grad = right_mmul(low_s[read], down_w[...])
            sigma = jax.nn.sigmoid(gate)
            inner_s[read] = (gate * sigma * up).astype(BF)
            grad_up = (inner_grad * gate * sigma).astype(BF)
            grad_gate = (inner_grad * up * sigma * (1.0 + gate * (1.0 - sigma))).astype(BF)
            gate_s[read] = grad_gate
            up_s[read] = grad_up
            total_back = mmul(grad_gate, gate_w[...]) + mmul(grad_up, up_w[...])
            back[span] = total_back.astype(BF)
            return carry

        lax.fori_loop(0, half // tile, body, 0)

    run(far_s, half)
    sends = [
        pltpu.make_async_copy(far_s.at[pl.ds(m * piece, piece)], back_far[m], far_sems.at[m])
        for m in range(chips)
    ]
    for send in sends:
        send.start()
    run(back_near, 0)
    for send in sends:
        send.wait()


def feed_grad_kernel(chips, line, *refs):
    hid, low, own, right, left, gate_s, up_s, inner_s, down_near, down_far, grads, *scratch = take(
        refs, 2 * chips, 2 * chips, None, line - 1, line - 1, *[None] * 4, chips, line, *[None] * 5
    )
    slots, down_w, hid_s, low_s, sems = scratch
    copies = load_all(hid, hid_s, sems) + load_all(low, low_s, sems.at[pl.ds(2 * chips, 2 * chips)])
    load_slots(own, right, left, slots)
    piece = hid[0].shape[0]
    units = own.shape[0] // 3
    for k in range(line):
        down_w[k * units : (k + 1) * units] = slots[k, 2 * units :]
    for copy in copies:
        copy.wait()
    half = chips * piece
    for m in range(chips):
        span = slice(m * piece, (m + 1) * piece)
        far = slice(half + m * piece, half + (m + 1) * piece)
        down_near[span] = mmul(inner_s[span], down_w[...]).astype(BF)
        down_far[m][...] = mmul(inner_s[far], down_w[...]).astype(BF)
    for n, (a, b) in enumerate(((gate_s, hid_s), (up_s, hid_s), (inner_s, low_s))):
        term = left_mmul(a[...], b[...])
        for k in range(line):
            out = term[k * units : (k + 1) * units]
            grads[k][n * units : (n + 1) * units] = out.astype(grads[k].dtype)


def middle_kernel(chips, line, *refs):
    parts, mid, out_grad, gain, attn, query, probs, cosine, sine, near, far, packets, *rest = take(
        refs, chips, *[None] * 8, chips, chips, line, *[None] * 4, line, *[None] * 4
    )
    grad_mid, gain_term, grad_low, grad_query, slots, low4, att3, grad_attn, grad_kv = rest
    s = lax.axis_index("seq")
    piece = mid.shape[0]
    cos, sin = tables(cosine, sine)
    grad = parts[0][...].astype(F32)
    for part in parts[1:]:
        grad = grad + part[...].astype(F32)
    x = mid[...]
    scale = rms_scale(x)
    back, term = norm_back(grad, x * scale, scale, gain[...])
    gain_term[...] = term
    whole = out_grad[...].T + back
    grad_mid[...] = whole
    low = whole.astype(BF)
    grad_low[...] = low
    split_lanes(low4, low, line)
    for ref, _, m, j in blocks(near, far):
        acc = 0.0
        for k in range(line):
            acc = acc + right_mmul(low4[s ^ k], ref[k, 1])
        att3[j] = acc.astype(BF)
    grad_attn[...] = join_lanes(att3, att3.shape[0])
    for g in range(KV_HEADS):
        keys = slot_rows(packets, piece, head_of(g))
        values = slot_rows(packets, piece, head_of(KV_HEADS + g))
        q = group_rows(query, g)
        ga = group_rows(grad_attn, g)
        at = group_rows(attn, g)
        dots = jnp.sum(ga.astype(F32) * at.astype(F32), -1, keepdims=True)
        weights = probs[g]
        gs = (weights * (right_mmul(ga, values) - dots) * INV_ROOT).astype(BF)
        gq = mmul(gs, keys)
        for i in range(GROUPS):
            u = gq[i * piece : (i + 1) * piece]
            h = GROUPS * g + i
            grad_query[:, head_of(h)] = (u * cos - swapped(u) * sin).astype(BF)
        grad_kv[:, head_of(g)] = left_mmul(gs, q)
        grad_kv[:, head_of(KV_HEADS + g)] = left_mmul(weights.astype(BF), ga)
    for k in range(line):
        slots[k][...] = grad_kv[k * piece : (k + 1) * piece].astype(slots[k].dtype)


def query_grad_kernel(chips, *refs):
    hidden, grad_query, attn, grad_low, near, far, out_near, out_far, back, *scratch = take(
        refs, *[None] * 4, chips, chips, chips, chips, *[None] * 5
    )
    hid3, att3, gq4, low4 = scratch
    line = near[0].shape[0]
    s = lax.axis_index("seq")
    size = hid3.shape[0]
    split_lanes(hid3, hidden[...], size)
    split_lanes(att3, attn[...], size)
    split_lanes(gq4, grad_query[...], line)
    split_lanes(low4, grad_low[...], line)
    for ref, core, m, j in blocks(near, far):
        out = (out_near, out_far)[core][m]
        for k in range(line):
            out[k, 0] = left_mmul(hid3[j], gq4[s ^ k]).astype(BF)
            out[k, 1] = left_mmul(att3[j], low4[s ^ k]).astype(BF)
    for ref, _, m, j in blocks(near, far):
        acc = 0.0
        for k in range(line):
            acc = acc + right_mmul(gq4[s ^ k], ref[k, 0])
        back[j] = acc


def input_grad_kernel(chips, line, *refs):
    parts, rows, gain, hidden, grad_mid, base, cosine, sine, feed_term, near, far, *rest = take(
        refs, line, *[None] * 8, chips, chips, None, 2 * chips, *[None] * 4
    )
    result, outs, hid3, full, gkv4, x3 = take(rest, *[None] * 6)
    cos, sin = tables(cosine, sine)
    s = lax.axis_index("seq")
    size = hid3.shape[0]
    both = parts[0][...]
    for part in parts[1:]:
        both = both + part[...].astype(F32)
    for h in range(KV_HEADS):
        u = both[:, head_of(h)]
        full[:, head_of(h)] = (u * cos - swapped(u) * sin).astype(BF)
    full[:, KV_WIDTH:] = both[:, KV_WIDTH:].astype(BF)
    wide = KV_WIDTH // line
    for p in range(line):
        gkv4[p, :, :wide] = full[:, p * wide : (p + 1) * wide]
        gkv4[p, :, wide:] = full[:, KV_WIDTH + p * wide : KV_WIDTH + (p + 1) * wide]
    split_lanes(hid3, hidden[...], size)
    for ref, _, m, j in blocks(near, far):
        acc = base[j]
        for k in range(line):
            acc = acc + right_mmul(gkv4[s ^ k], ref[k])
        x3[j] = acc
    x = rows[...].T
    scale = rms_scale(x)
    back, term = norm_back(join_lanes(x3, size), x * scale, scale, gain[...])
    result[...] = (grad_mid[...] + back).T
    rows_of = hid3.shape[2]
    lanes = 2 * wide
    each = x.shape[1] // lanes
    for ref, core, m, j in blocks(near, far):
        out = outs[core * chips + m]
        for k in range(line):
            span = slice(k * rows_of, (k + 1) * rows_of)
            out[span] = left_mmul(hid3[j], gkv4[s ^ k]).astype(BF)
        base_row = line * rows_of
        out[base_row:] = jnp.zeros((out.shape[0] - base_row, lanes), BF)
        for n, value in enumerate((term, feed_term[...])):
            for i in range(each):
                at = base_row + n * each + i
                out[at : at + 1] = value[:, i * lanes : (i + 1) * lanes].astype(BF)


def join_kernel(key, value, query, output, out):
    a = key.shape[0]
    b = query.shape[1]
    out[:, :a] = key[...].T
    out[:, a : 2 * a] = value[...].T
    out[:, 2 * a : 2 * a + b] = query[...]
    out[:, 2 * a + b :] = output[...]


def stack_kernel(line, *refs):
    slots, kv, qo = take(refs, line, None, None)
    a = kv.shape[2]
    b = qo.shape[3]
    for k in range(line):
        kv[k] = slots[k][:, :a]
        qo[k, 0] = slots[k][:, a : a + b]
        qo[k, 1] = slots[k][:, a + b :]


def cast_kernel(grad, out):
    out[...] = grad[...].T.astype(BF)


def spread_kernel(gate, up, down, out):
    units = out.shape[2]
    for j in range(out.shape[0]):
        span = slice(j * units, (j + 1) * units)
        out[j, 0] = gate[:, span].T
        out[j, 1] = up[:, span].T
        out[j, 2] = down[:, span].T


def arrange_kernel(got, out):
    cut = got.shape[3]
    units = got.shape[2]
    for j in range(got.shape[0]):
        for n in range(3):
            out[n * units : (n + 1) * units, j * cut : (j + 1) * cut] = got[j, n]


def pair_sum_kernel(chips, *refs):
    near, got, own, outs = take(refs, chips, chips, None, chips - 1)
    own[...] = near[0][...].astype(F32) + got[0][...].astype(F32)
    for m in range(1, chips):
        outs[m - 1][...] = (near[m][...].astype(F32) + got[m][...].astype(F32)).astype(BF)


def stack_sum_kernel(chips, near, *refs):
    got, own, outs = take(refs, chips, None, chips - 1)
    rows = own.shape[0]
    own[...] = near[:rows].astype(F32) + got[0][...].astype(F32)
    for m in range(1, chips):
        mine = near[m * rows : (m + 1) * rows].astype(F32)
        outs[m - 1][...] = (mine + got[m][...].astype(F32)).astype(BF)


def down_end_kernel(mid, own, *refs):
    *got, out = refs
    out[...] = (mid[...] + tree([own[...]] + [g[...].astype(F32) for g in got])).T


def feed_end_kernel(own, *refs):
    *got, out = refs
    whole = tree([own[...]] + [g[...].astype(F32) for g in got]).astype(BF)
    split_lanes(out, whole, out.shape[0])


def feed_done_kernel(got, gate, up, down):
    units = got.shape[2]
    for j in range(got.shape[0]):
        span = slice(j * units, (j + 1) * units)
        gate[:, span] = got[j, 0].astype(F32).T
        up[:, span] = got[j, 1].astype(F32).T
        down[:, span] = got[j, 2].astype(F32).T


def qo_line_kernel(chips, own, *refs):
    got, mine, sent = take(refs, chips - 1, None, len(refs) - chips)
    for k in range(own.shape[0]):
        whole = tree([own[k]] + [g[k].astype(F32) for g in got])
        if k == 0:
            mine[...] = whole
        else:
            sent[k - 1][...] = whole.astype(BF)


def qo_end_kernel(own, *refs):
    *got, query, output = refs
    query[...] = tree([own[0]] + [g[0].astype(F32) for g in got])
    output[...] = tree([own[1]] + [g[1].astype(F32) for g in got])


def kv_line_kernel(chips, line, own, *refs):
    got, mine, gains, sent = take(refs, chips - 1, None, None, line - 1)
    cut = mine.shape[0]
    last = slice(line * cut, None)
    term = tree([own[last].astype(BF).astype(F32)] + [g[last].astype(F32) for g in got]).astype(BF)
    gains[...] = term.astype(F32)
    for k in range(line):
        span = slice(k * cut, (k + 1) * cut)
        whole = tree([own[span]] + [g[span].astype(F32) for g in got])
        if k == 0:
            mine[...] = whole
        else:
            sent[k - 1][:cut] = whole.astype(BF)
            sent[k - 1][cut:] = term


def kv_end_kernel(line, own, own_gains, *refs):
    got, keys, values, attn_gain, feed_gain = take(refs, line - 1, *[None] * 4)
    cut, lanes = own.shape
    whole = tree([own[...]] + [g[:cut].astype(F32) for g in got])
    keys[...] = whole[:, : lanes // 2].T
    values[...] = whole[:, lanes // 2 :].T
    gains = tree([own_gains[...]] + [g[cut:].astype(F32) for g in got])
    each = attn_gain.shape[1] // lanes
    for n, out in enumerate((attn_gain, feed_gain)):
        for i in range(each):
            out[:, i * lanes : (i + 1) * lanes] = gains[n * each + i : n * each + i + 1]


def padded(a):
    if len(a.shape) < 2:
        return 4096
    size = jnp.dtype(a.dtype).itemsize
    *outer, rows, lanes = a.shape
    tile = 32 // size
    return math.prod(outer) * (-(-rows // tile) * tile) * (-(-lanes // 128) * 128) * size


def call(kernel, outs, scratch, flops, *args, far=0, far_outs=(), room=None):
    sizes = [a.size * a.dtype.itemsize for a in (*args, *outs)]
    vmem = pl.BlockSpec(memory_space=pltpu.VMEM)
    free = pl.BlockSpec(memory_space=pl.ANY)
    limit = None
    if room is not None:
        limit = sum(padded(a) for a in (*args, *outs)) + room * 2**20
    return pl.pallas_call(
        kernel,
        out_shape=outs,
        in_specs=[free if i < far else vmem for i in range(len(args))],
        out_specs=[free if i in far_outs else vmem for i in range(len(outs))],
        scratch_shapes=[x if not isinstance(x, tuple) else pltpu.VMEM(x[0], x[1]) for x in scratch],
        cost_estimate=pl.CostEstimate(
            flops=int(flops), bytes_accessed=sum(sizes), transcendentals=0
        ),
        compiler_params=pltpu.CompilerParams(vmem_limit_bytes=limit),
    )(*args)


def array(shape, dtype):
    return jax.ShapeDtypeStruct(shape, dtype)


def flip(x, bits):
    n = lax.axis_size("batch")
    return lax.ppermute(x, "batch", [(i, i ^ bits) for i in range(n)])


def cross(x, bits):
    n = lax.axis_size("seq")
    return lax.ppermute(x, "seq", [(i, i ^ bits) for i in range(n)])


def push(x, by):
    n = lax.axis_size("seq")
    pairs = [(i, i + by) for i in range(n) if 0 <= i + by < n]
    return lax.ppermute(x, "seq", pairs)


def tree(terms):
    while len(terms) > 1:
        terms = [terms[i] + terms[i + 1] for i in range(0, len(terms), 2)]
    return terms[0]


def plane_hops(x, chips):
    return [x] + [flip(x, 2 * m) for m in range(1, chips)]


def pair_swap(xs):
    return [flip(x, 1) for x in xs]


def plane_sum(near, far, chips):
    got = pair_swap(far)
    block = far[0].shape
    one = not isinstance(near, (list, tuple))
    own, *low = call(
        functools.partial(stack_sum_kernel if one else pair_sum_kernel, chips),
        [array(block, F32)] + [array(block, BF)] * (chips - 1),
        [],
        1e6,
        *([near] if one else near),
        *got,
    )
    return own, [flip(low[m - 1], 2 * m) for m in range(1, chips)]


def line_chain(x, line):
    out = []
    for by in (1, -1):
        held = x
        got = []
        for k in range(1, line):
            held = step(held, by, k)
            got.append(held)
        out.append(got)
    return out


def step(x, by, k):
    n = lax.axis_size("seq")
    senders = range(k - 1, n - 1) if by > 0 else range(1, n - k + 1)
    return lax.ppermute(x, "seq", [(i, i + by) for i in senders])


def shards(
    activations,
    segment_ids,
    attention_gain,
    query_weight,
    key_weight,
    value_weight,
    output_weight,
    feed_gain,
    gate_weight,
    up_weight,
    down_weight,
    out_grad,
):
    piece, width = activations.shape[1:]
    line = lax.axis_size("seq")
    size = lax.axis_size("batch")
    length = piece * line
    chips = size // 2
    cut = width // size
    rows = activations[0].T
    grad_rows = out_grad[0].T
    s = lax.axis_index("seq")
    positions = s * piece + jnp.arange(piece, dtype=jnp.int32)
    cosine, sine = rotary_tables(positions.astype(F32))
    gain_attn = attention_gain[None]
    gain_feed = feed_gain[None]
    units = gate_weight.shape[1] // size
    others = range(1, line)

    kv_cols = 2 * key_weight.shape[1]
    qo_cols = query_weight.shape[1]
    (own,) = call(
        join_kernel,
        [array((cut, kv_cols + 2 * qo_cols), BF)],
        [],
        1e5,
        key_weight.T,
        value_weight.T,
        query_weight,
        output_weight,
    )
    kv_slots, qo_slots = call(
        functools.partial(stack_kernel, line),
        [array((line, cut, kv_cols), BF), array((line, 2, cut, qo_cols), BF)],
        [],
        1e5,
        own,
        *[cross(own, k) for k in others],
        room=ROOM,
    )
    kv_near = plane_hops(kv_slots, chips)
    kv_far = pair_swap(kv_near)
    qo_near = plane_hops(qo_slots, chips)
    qo_far = pair_swap(qo_near)

    (local,) = call(
        spread_kernel,
        [array((size, 3, units, cut), BF)],
        [],
        1e5,
        gate_weight,
        up_weight,
        down_weight.T,
    )
    spread = lax.all_to_all(local, "batch", split_axis=0, concat_axis=0, tiled=True)
    (feed_own,) = call(arrange_kernel, [array((3 * units, width), BF)], [], 1e5, spread, room=ROOM)
    feed_right, feed_left = line_chain(feed_own, line)

    (low,) = call(cast_kernel, [array((piece, width), BF)], [], 1e5, grad_rows)
    low_near = plane_hops(low, chips)
    low_far = pair_swap(low_near)

    hidden_attn, packet = call(
        functools.partial(kv_kernel, chips),
        [array((piece, width), BF), array((piece + 8, 2 * KV_WIDTH), BF)],
        [((size, piece, cut), BF), ((line, piece, kv_cols), F32)],
        2 * piece * width * 2 * KV_WIDTH,
        rows,
        gain_attn,
        cosine,
        sine,
        segment_ids,
        *kv_near,
        *kv_far,
    )
    packets = [packet] + [push(packet, k) for k in others]
    (query,) = call(
        functools.partial(query_kernel, chips),
        [array((piece, width), BF)],
        [((size, piece, cut), BF), ((line, piece, qo_cols), F32)],
        2 * piece * width * width,
        hidden_attn,
        cosine,
        sine,
        *qo_near,
        *qo_far,
    )
    probs, attn, mid, hidden_feed = call(
        functools.partial(attention_kernel, chips, line),
        [
            array((KV_HEADS, GROUPS * piece, length), F32),
            array((piece, width), BF),
            array((piece, width), F32),
            array((piece, width), BF),
        ],
        [((piece, length), F32), ((size, piece, cut), BF), ((line, piece, qo_cols), F32)],
        2 * piece * width * (width + 2 * length),
        query,
        *packets,
        rows,
        segment_ids,
        gain_feed,
        *qo_near,
        *qo_far,
    )
    hid_near = plane_hops(hidden_feed, chips)
    hid_far = pair_swap(hid_near)
    flat = (chips * piece, width)
    tokens = size * piece
    act = (tokens, line * units)
    feed_in = [*hid_near, *hid_far, *low_near, *low_far, feed_own, *feed_right, *feed_left]
    slots = [((line, 3 * units, width), BF), ((line * units, width), BF)]
    both = [((tokens, width), BF)] * 2
    sems = pltpu.SemaphoreType.DMA((4 * chips,))
    back_near, *rest = call(
        functools.partial(feed_kernel, chips, line, 2 * piece),
        [array(flat, BF)] + [array((piece, width), BF)] * chips + [array(act, BF)] * 3,
        [
            slots[0],
            slots[1],
            slots[1],
            slots[1],
            *both,
            (flat, BF),
            sems,
            pltpu.SemaphoreType.DMA((chips,)),
        ],
        10 * tokens * width * line * units,
        *feed_in,
        far=len(feed_in),
        far_outs=range(1, chips + 1),
    )
    back_far, acts = rest[:chips], rest[chips:]
    back_own, back_got = plane_sum(back_near, back_far, chips)
    down_near, *rest = call(
        functools.partial(feed_grad_kernel, chips, line),
        [array(flat, BF)]
        + [array((piece, width), BF)] * chips
        + [array((3 * units, width), F32)]
        + [array((3 * units, width), BF)] * (line - 1),
        [*slots, *both, sems],
        8 * tokens * width * line * units,
        *feed_in,
        *acts,
        far=len(feed_in),
    )
    down_far, feed_grads = rest[:chips], rest[chips:]
    grad_mid, feed_term, grad_mid_low, grad_query, kv_own, *kv_sent = call(
        functools.partial(middle_kernel, chips, line),
        [
            array((piece, width), F32),
            array((1, width), F32),
            array((piece, width), BF),
            array((piece, width), BF),
            array((piece, 2 * KV_WIDTH), F32),
        ]
        + [array((piece, 2 * KV_WIDTH), BF)] * (line - 1),
        [
            ((line, piece, qo_cols), BF),
            ((size, piece, cut), BF),
            ((piece, width), BF),
            ((length, 2 * KV_WIDTH), F32),
        ],
        2 * piece * width * (width + 4 * length),
        back_own,
        *back_got,
        mid,
        grad_rows,
        gain_feed,
        attn,
        query,
        probs,
        cosine,
        sine,
        *qo_near,
        *qo_far,
        *packets,
    )
    kv_got = [push(kv_sent[k - 1], -k) for k in others]

    down_own, down_got = plane_sum(down_near, down_far, chips)
    (block_output,) = call(
        down_end_kernel, [array((width, piece), F32)], [], 1e6, mid, down_own, *down_got, room=ROOM
    )

    feed_got = [cross(feed_grads[k], k) for k in others]
    (feed_own,) = call(
        feed_end_kernel,
        [array((size, 3 * units, cut), BF)],
        [],
        1e6,
        feed_grads[0],
        *feed_got,
        room=ROOM,
    )
    feed_back = lax.all_to_all(feed_own, "batch", split_axis=0, concat_axis=0, tiled=True)
    gate_done, up_done, down_done = call(
        feed_done_kernel,
        [
            array(gate_weight.shape, F32),
            array(up_weight.shape, F32),
            array(down_weight.shape[::-1], F32),
        ],
        [],
        1e6,
        feed_back.reshape(size, 3, units, cut),
        room=ROOM,
    )

    shape = (line, 2, cut, qo_cols)
    *qo_grads, base = call(
        functools.partial(query_grad_kernel, chips),
        [array(shape, BF)] * size + [array((size, piece, cut), F32)],
        [((size, piece, cut), BF)] * 2 + [((line, piece, qo_cols), BF)] * 2,
        6 * piece * width * width,
        hidden_attn,
        grad_query,
        attn,
        grad_mid_low,
        *qo_near,
        *qo_far,
    )
    qo_own, qo_got = plane_sum(qo_grads[:chips], qo_grads[chips:], chips)
    block = (2, cut, qo_cols)
    qo_own, *qo_sent = call(
        functools.partial(qo_line_kernel, chips),
        [array(block, F32)] + [array(block, BF)] * (line - 1),
        [],
        1e6,
        qo_own,
        *qo_got,
        room=ROOM,
    )
    qo_got = [cross(qo_sent[k - 1], k) for k in others]
    query_done, output_done = call(
        qo_end_kernel, [array((cut, qo_cols), F32)] * 2, [], 1e6, qo_own, *qo_got, room=ROOM
    )

    each = width // kv_cols
    extra = -(-2 * each // 16) * 16
    shape = (line * cut + extra, kv_cols)
    input_grad, *kv_grads = call(
        functools.partial(input_grad_kernel, chips, line),
        [array((width, piece), F32)] + [array(shape, BF)] * size,
        [
            ((size, piece, cut), BF),
            ((piece, 2 * KV_WIDTH), BF),
            ((line, piece, kv_cols), BF),
            ((size, piece, cut), F32),
        ],
        4 * piece * width * 2 * KV_WIDTH,
        kv_own,
        *kv_got,
        rows,
        gain_attn,
        hidden_attn,
        grad_mid,
        base,
        cosine,
        sine,
        feed_term,
        *kv_near,
        *kv_far,
    )
    kv_own, kv_got = plane_sum(kv_grads[:chips], kv_grads[chips:], chips)
    kv_own, own_gains, *kv_sent = call(
        functools.partial(kv_line_kernel, chips, line),
        [array((cut, kv_cols), F32), array((extra, kv_cols), F32)]
        + [array((cut + extra, kv_cols), BF)] * (line - 1),
        [],
        1e6,
        kv_own,
        *kv_got,
        room=ROOM,
    )
    kv_got = [cross(kv_sent[k - 1], k) for k in others]
    key_done, value_done, attn_gain_sum, feed_gain_sum = call(
        functools.partial(kv_end_kernel, line),
        [array((kv_cols // 2, cut), F32)] * 2 + [array((1, width), F32)] * 2,
        [],
        1e6,
        kv_own,
        own_gains,
        *kv_got,
        room=ROOM,
    )
    return (
        block_output.T[None],
        input_grad.T[None],
        attn_gain_sum[0],
        query_done,
        key_done.T,
        value_done.T,
        output_done,
        feed_gain_sum[0],
        gate_done,
        up_done,
        down_done.T,
    )


def solution(mesh):
    both = P("batch", "seq")
    tokens = P("batch", "seq", None)
    in_specs = (tokens, both, P(), both, both, both, both, P(), both, both, P("seq", "batch"), tokens)
    out_specs = (tokens, tokens, P(), both, both, both, both, P(), both, both, P("seq", "batch"))

    return jax.shard_map(shards, mesh=mesh, in_specs=in_specs, out_specs=out_specs, check_vma=False)
```

profile of v0, /device:TPU:0, one launch (start us, length us, event | category | flops | bytes accessed | tf_op | source)
XLA Modules:
  0.0 315.8 jit_solution(12251940631008294387)
XLA Ops:
  2.4 5.1 %collective-permute-start.2 = (bf16[120,640]{1,0:T(8,128)(2,1)}, bf16[120,640]{1,0:T(8,128)(2,1)S(1)}, u32[]{:S(2)}, u32[]{:S(2)}) collective-permute-start(bf16[120,640]{1,0:T(8,128)(2,1)} %shard_map.203.refs_0_), channel_id=1, source_target_pairs={{0,3},{1,2},{2,1},{3,0},{4,7},{5,6},{6,5},{7,4},{8,11},{9,10},{10,... | collective-permute-start | bytes 460808 | tf_op jit(solution)/shard_map/ppermute | solution.py:567
  12.6 8.1 %collective-permute-done.1.refs_2_ = bf16[120,640]{1,0:T(8,128)(2,1)S(1)} collective-permute-done((bf16[120,640]{1,0:T(8,128)(2,1)}, bf16[120,640]{1,0:T(8,128)(2,1)S(1)}, u32[]{:S(2)}, u32[]{:S(2)}) %collective-permute-start.1) | collective-permute-done | bytes 153632 | tf_op jit(solution)/shard_map/ppermute | solution.py:567
  25.4 6.3 %collective-permute-done.5.refs_8_.refs_15_ = bf16[4,120,160]{2,1,0:T(8,128)(2,1)S(1)} collective-permute-done((bf16[4,120,160]{2,1,0:T(8,128)(2,1)S(1)}, bf16[4,120,160]{2,1,0:T(8,128)(2,1)S(1)}, u32[]{:S(2)}, u32[]{:S(2)}) %collective-permute-start.5) | collective-permute-done | bytes 153632 | tf_op jit(solution)/shard_map/ppermute | solution.py:562
  50.1 4.0 %shard_map.205 = (bf16[128,960]{1,0:T(8,128)(2,1)}, bf16[136,640]{1,0:T(8,128)(2,1)}) custom-call(f32[960,128]{1,0:T(8,128)} %bitcast.24, f32[1,960]{1,0:T(1,128)} %bitcast.35, f32[128,32]{1,0:T(8,128)} %get-tuple-element.182.refs_2_.refs_1_.refs_10_.refs_9_, f32[128,32]{1,0:T(8,128)} %get-tuple-element.181.refs_3_.refs_2_.refs_11_.refs_10_, ...), custom_call_target="tpu_custom_call" | custom-call | flops 157286400 | bytes 2177280 | tf_op jit(solution)/shard_map/pallas_call | solution.py:543
  54.1 14.0 %collective-permute-done.29.refs_11_ = bf16[128,960]{1,0:T(8,128)(2,1)} collective-permute-done((bf16[128,960]{1,0:T(8,128)(2,1)}, bf16[128,960]{1,0:T(8,128)(2,1)}, u32[]{:S(2)}, u32[]{:S(2)}) %collective-permute-start.29) | collective-permute-done | bytes 245792 | tf_op jit(solution)/shard_map/ppermute | solution.py:562
  68.1 4.9 %collective-permute-start.19 = (bf16[136,640]{1,0:T(8,128)(2,1)}, bf16[136,640]{1,0:T(8,128)(2,1)}, u32[]{:S(2)}, u32[]{:S(2)}) collective-permute-start(bf16[136,640]{1,0:T(8,128)(2,1)} %get-tuple-element.99.refs_1_.refs_20_), channel_id=1, source_target_pairs={{0,3},{4,7},{8,11},{12,15},{16,19},{20,23},{24,27},{28,31}} | collective-permute-start | bytes 522248 | tf_op jit(solution)/shard_map/ppermute | solution.py:573
  79.0 5.3 %collective-permute-start.34 = (bf16[240,960]{1,0:T(8,128)(2,1)S(1)}, bf16[240,960]{1,0:T(8,128)(2,1)}, u32[]{:S(2)}, u32[]{:S(2)}) collective-permute-start(bf16[240,960]{1,0:T(8,128)(2,1)S(1)} %shard_map.210.refs_16_), channel_id=1, source_target_pairs={{0,1},{1,2},{2,3},{4,5},{5,6},{6,7},{8,9},{9,10},{10,11},{12,13},{... | collective-permute-start | bytes 1382408 | tf_op jit(solution)/shard_map/ppermute | solution.py:620
  85.0 6.8 %collective-permute-done.37.refs_20_ = bf16[240,960]{1,0:T(8,128)(2,1)} collective-permute-done((bf16[240,960]{1,0:T(8,128)(2,1)S(1)}, bf16[240,960]{1,0:T(8,128)(2,1)}, u32[]{:S(2)}, u32[]{:S(2)}) %collective-permute-start.37) | collective-permute-done | bytes 460832 | tf_op jit(solution)/shard_map/ppermute | solution.py:620
  98.4 4.4 %shard_map.206.refs_0_.refs_8_ = bf16[128,960]{1,0:T(8,128)(2,1)} custom-call(bf16[128,960]{1,0:T(8,128)(2,1)} %get-tuple-element.97.refs_0_.refs_6_, f32[128,32]{1,0:T(8,128)} %get-tuple-element.182.refs_2_.refs_1_.refs_10_.refs_9_, f32[128,32]{1,0:T(8,128)} %get-tuple-element.181.refs_3_.refs_2_.refs_11_.refs_10_, bf16[4,2,120,240]{3,2,1,0:T(8,128)(2,1)} %copy-done, ...), custom_call_target="tpu_custom_call" | custom-call | flops 235929600 | bytes 4210688 | tf_op jit(solution)/shard_map/pallas_call | solution.py:543
  102.8 8.5 %shard_map.207 = (f32[5,384,512]{2,1,0:T(8,128)}, bf16[128,960]{1,0:T(8,128)(2,1)}, f32[128,960]{1,0:T(8,128)}, bf16[128,960]{1,0:T(8,128)(2,1)}) custom-call(bf16[128,960]{1,0:T(8,128)(2,1)} %shard_map.206.refs_0_.refs_8_, bf16[136,640]{1,0:T(8,128)(2,1)} %get-tuple-element.99.refs_1_.refs_20_, bf16[136,640]{1,0:T(8,128)(2,1)} %collective-permute-done.17.refs_2_.refs_21_, ...), custom_call_target="tpu_custom_call" | custom-call | flops 487587840 | bytes 10039552 | tf_op jit(solution)/shard_map/pallas_call | solution.py:543
  118.5 4.8 %collective-permute-done.22.refs_3_ = bf16[128,960]{1,0:T(8,128)(2,1)S(1)} collective-permute-done((bf16[128,960]{1,0:T(8,128)(2,1)}, bf16[128,960]{1,0:T(8,128)(2,1)S(1)}, u32[]{:S(2)}, u32[]{:S(2)}) %collective-permute-start.22) | collective-permute-done | bytes 245792 | tf_op jit(solution)/shard_map/ppermute | solution.py:562
  123.4 4.4 %collective-permute-done.21.refs_2_ = bf16[128,960]{1,0:T(8,128)(2,1)S(1)} collective-permute-done((bf16[128,960]{1,0:T(8,128)(2,1)}, bf16[128,960]{1,0:T(8,128)(2,1)S(1)}, u32[]{:S(2)}, u32[]{:S(2)}) %collective-permute-start.21) | collective-permute-done | bytes 245792 | tf_op jit(solution)/shard_map/ppermute | solution.py:562
  129.7 7.8 %collective-permute-done.39.refs_22_ = bf16[240,960]{1,0:T(8,128)(2,1)S(1)} collective-permute-done((bf16[240,960]{1,0:T(8,128)(2,1)}, bf16[240,960]{1,0:T(8,128)(2,1)S(1)}, u32[]{:S(2)}, u32[]{:S(2)}) %collective-permute-start.39) | collective-permute-done | bytes 460832 | tf_op jit(solution)/shard_map/ppermute | solution.py:620
  139.1 14.0 %shard_map.211 = (bf16[512,960]{1,0:T(8,128)(2,1)}, bf16[128,960]{1,0:T(8,128)(2,1)}, bf16[128,960]{1,0:T(8,128)(2,1)}, bf16[128,960]{1,0:T(8,128)(2,1)}, bf16[1...) custom-call(bf16[128,960]{1,0:T(8,128)(2,1)} %get-tuple-element.101.refs_, ...), custom_call_target="tpu_custom_call" | custom-call | flops 3145728000 | bytes 11089920 | tf_op jit(solution)/shard_map/pallas_call | solution.py:543
  154.2 12.0 %shard_map.212 = (bf16[512,960]{1,0:T(8,128)(2,1)}, bf16[128,960]{1,0:T(8,128)(2,1)}, bf16[128,960]{1,0:T(8,128)(2,1)}, bf16[128,960]{1,0:T(8,128)(2,1)}, bf16[1...) custom-call(bf16[128,960]{1,0:T(8,128)(2,1)} %get-tuple-element.101., ...), custom_call_target="tpu_custom_call" | custom-call | flops 2516582400 | bytes 13393920 | tf_op jit(solution)/shard_map/pallas_call | solution.py:543
  179.4 6.3 %collective-permute-done.52.refs_2_ = bf16[128,960]{1,0:T(8,128)(2,1)S(1)} collective-permute-done((bf16[128,960]{1,0:T(8,128)(2,1)}, bf16[128,960]{1,0:T(8,128)(2,1)S(1)}, u32[]{:S(2)}, u32[]{:S(2)}) %collective-permute-start.52) | collective-permute-done | bytes 245792 | tf_op jit(solution)/shard_map/ppermute | solution.py:562
  186.5 10.1 %shard_map.216 = (f32[128,960]{1,0:T(8,128)}, f32[1,960]{1,0:T(1,128)}, bf16[128,960]{1,0:T(8,128)(2,1)}, bf16[128,960]{1,0:T(8,128)(2,1)}, f32[128,640]{1,0:T(8...) custom-call(f32[128,960]{1,0:T(8,128)} %get-tuple-element.119.refs_0_, ...), custom_call_target="tpu_custom_call" | custom-call | flops 739246080 | bytes 12860928 | tf_op jit(solution)/shard_map/pallas_call | solution.py:543
  196.6 6.4 %shard_map.217 = (bf16[4,2,120,240]{3,2,1,0:T(8,128)(2,1)}, bf16[4,2,120,240]{3,2,1,0:T(8,128)(2,1)}, bf16[4,2,120,240]{3,2,1,0:T(8,128)(2,1)}, bf16[4,2,120,240...) custom-call(bf16[128,960]{1,0:T(8,128)(2,1)} %get-tuple-element.97.r, ...), custom_call_target="tpu_custom_call" | custom-call | flops 707788800 | bytes 8847360 | tf_op jit(solution)/shard_map/pallas_call | solution.py:543
  206.0 4.9 %collective-permute-done.78.refs_1_ = bf16[240,960]{1,0:T(8,128)(2,1)S(1)} collective-permute-done((bf16[240,960]{1,0:T(8,128)(2,1)}, bf16[240,960]{1,0:T(8,128)(2,1)S(1)}, u32[]{:S(2)}, u32[]{:S(2)}) %collective-permute-start.78) | collective-permute-done | bytes 460832 | tf_op jit(solution)/shard_map/ppermute | solution.py:567
  223.9 5.5 %collective-permute-done.54.refs_1_ = bf16[128,640]{1,0:T(8,128)(2,1)} collective-permute-done((bf16[128,640]{1,0:T(8,128)(2,1)}, bf16[128,640]{1,0:T(8,128)(2,1)}, u32[]{:S(2)}, u32[]{:S(2)}) %collective-permute-start.54) | collective-permute-done | bytes 163872 | tf_op jit(solution)/shard_map/ppermute | solution.py:573
  229.9 17.2 %collective-permute-done.55.refs_2_ = bf16[128,640]{1,0:T(8,128)(2,1)} collective-permute-done((bf16[128,640]{1,0:T(8,128)(2,1)}, bf16[128,640]{1,0:T(8,128)(2,1)}, u32[]{:S(2)}, u32[]{:S(2)}) %collective-permute-start.55) | collective-permute-done | bytes 163872 | tf_op jit(solution)/shard_map/ppermute | solution.py:573
  249.3 5.4 %shard_map.218 = (f32[960,128]{1,0:T(8,128)}, bf16[496,160]{1,0:T(8,128)(2,1)}, bf16[496,160]{1,0:T(8,128)(2,1)}, bf16[496,160]{1,0:T(8,128)(2,1)}, bf16[496,160...) custom-call(f32[128,640]{1,0:T(8,128)} %get-tuple-element.125.refs_0, ...), custom_call_target="tpu_custom_call" | custom-call | flops 314572800 | bytes 5570048 | tf_op jit(solution)/shard_map/pallas_call | solution.py:543
  270.8 8.6 %collective-permute-done.72.refs_1_ = bf16[4,2,120,240]{3,2,1,0:T(8,128)(2,1)S(1)} collective-permute-done((bf16[4,2,120,240]{3,2,1,0:T(8,128)(2,1)}, bf16[4,2,120,240]{3,2,1,0:T(8,128)(2,1)S(1)}, u32[]{:S(2)}, u32[]{:S(2)}) %collective-permute-start.72) | collective-permute-done | bytes 460832 | tf_op jit(solution)/shard_map/ppermute | solution.py:562
  284.5 13.0 %collective-permute-done.62.refs_1_ = bf16[496,160]{1,0:T(8,128)(2,1)S(1)} collective-permute-done((bf16[496,160]{1,0:T(8,128)(2,1)}, bf16[496,160]{1,0:T(8,128)(2,1)S(1)}, u32[]{:S(2)}, u32[]{:S(2)}) %collective-permute-start.62) | collective-permute-done | bytes 158752 | tf_op jit(solution)/shard_map/ppermute | solution.py:562
  (271 shorter events, 126.7 us)
Async XLA Ops:
  9.9 32.1 %collective-permute-start.30 = (bf16[128,960]{1,0:T(8,128)(2,1)}, bf16[128,960]{1,0:T(8,128)(2,1)S(1)}, u32[]{:S(2)}, u32[]{:S(2)}) collective-permute-start(bf16[128,960]{1,0:T(8,128)(2,1)} %shard_map.208.refs_8_), channel_id=1, source_target_pairs={{0,4},{4,0},{8,12},{12,8},{16,20},{20,16},{24,28},{28,24},{1,5},{5... | collective-permute-start | bytes 737288 | tf_op jit(solution)/shard_map/ppermute | solution.py:562
  38.5 38.9 %all-to-all-start = ((bf16[8,3,80,120]{3,2,1,0:T(8,128)(2,1)}), bf16[8,3,80,120]{3,2,1,0:T(8,128)(2,1)S(1)}, u32[]{:S(2)}, u32[]{:S(2)}) async-start(bf16[8,3,80,120]{3,2,1,0:T(8,128)(2,1)} %shard_map.209), calls=%async_computation | async-start | bytes 983040 | tf_op jit(solution)/shard_map/all_to_all | solution.py:688
  42.0 31.0 %collective-permute-start.13 = (bf16[4,2,120,240]{3,2,1,0:T(8,128)(2,1)S(1)}, bf16[4,2,120,240]{3,2,1,0:T(8,128)(2,1)S(1)}, u32[]{:S(2)}, u32[]{:S(2)}) collective-permute-start(bf16[4,2,120,240]{3,2,1,0:T(8,128)(2,1)S(1)} %get-tuple-element.98.refs_3_.refs_8_.refs_12_.refs_4_), channel_id=1, source_target_pairs={{0,4},{4,0},{8,12},{12,8},{16,20},{20,16},{24,28},{28,24},{1,5},{5... | collective-permute-start | bytes 1382408 | tf_op jit(solution)/shard_map/ppermute | solution.py:562
  42.7 32.2 %collective-permute-start.12 = (bf16[4,2,120,240]{3,2,1,0:T(8,128)(2,1)S(1)}, bf16[4,2,120,240]{3,2,1,0:T(8,128)(2,1)S(1)}, u32[]{:S(2)}, u32[]{:S(2)}) collective-permute-start(bf16[4,2,120,240]{3,2,1,0:T(8,128)(2,1)S(1)} %get-tuple-element.98.refs_3_.refs_8_.refs_12_.refs_4_), channel_id=1, source_target_pairs={{0,24},{4,28},{8,16},{12,20},{16,8},{20,12},{24,0},{28,4},{1,25},{... | collective-permute-start | bytes 1382408 | tf_op jit(solution)/shard_map/ppermute | solution.py:562
  45.6 22.5 %collective-permute-start.29 = (bf16[128,960]{1,0:T(8,128)(2,1)}, bf16[128,960]{1,0:T(8,128)(2,1)}, u32[]{:S(2)}, u32[]{:S(2)}) collective-permute-start(bf16[128,960]{1,0:T(8,128)(2,1)} %shard_map.208.refs_8_), channel_id=1, source_target_pairs={{0,24},{4,28},{8,16},{12,20},{16,8},{20,12},{24,0},{28,4},{1,25},{... | collective-permute-start | bytes 737288 | tf_op jit(solution)/shard_map/ppermute | solution.py:562
  46.3 31.5 %collective-permute-start.11 = (bf16[4,2,120,240]{3,2,1,0:T(8,128)(2,1)S(1)}, bf16[4,2,120,240]{3,2,1,0:T(8,128)(2,1)S(1)}, u32[]{:S(2)}, u32[]{:S(2)}) collective-permute-start(bf16[4,2,120,240]{3,2,1,0:T(8,128)(2,1)S(1)} %get-tuple-element.98.refs_3_.refs_8_.refs_12_.refs_4_), channel_id=1, source_target_pairs={{0,16},{4,20},{8,24},{12,28},{16,0},{20,4},{24,8},{28,12},{1,17},{... | collective-permute-start | bytes 1382408 | tf_op jit(solution)/shard_map/ppermute | solution.py:562
  47.7 31.4 %collective-permute-start.10 = (bf16[4,2,120,240]{3,2,1,0:T(8,128)(2,1)S(1)}, bf16[4,2,120,240]{3,2,1,0:T(8,128)(2,1)}, u32[]{:S(2)}, u32[]{:S(2)}) collective-permute-start(bf16[4,2,120,240]{3,2,1,0:T(8,128)(2,1)S(1)} %get-tuple-element.98.refs_3_.refs_8_.refs_12_.refs_4_), channel_id=1, source_target_pairs={{0,8},{4,12},{8,0},{12,4},{16,24},{20,28},{24,16},{28,20},{1,9},{5... | collective-permute-start | bytes 1382408 | tf_op jit(solution)/shard_map/ppermute | solution.py:562
  95.6 20.9 %collective-permute-start.38 = (bf16[240,960]{1,0:T(8,128)(2,1)}, bf16[240,960]{1,0:T(8,128)(2,1)}, u32[]{:S(2)}, u32[]{:S(2)}) collective-permute-start(bf16[240,960]{1,0:T(8,128)(2,1)} %collective-permute-done.37.refs_20_), channel_id=1, source_target_pairs={{1,0},{2,1},{5,4},{6,5},{9,8},{10,9},{13,12},{14,13},{17,16},{18,1... | collective-permute-start | bytes 1382408 | tf_op jit(solution)/shard_map/ppermute | solution.py:620
  116.5 21.0 %collective-permute-start.39 = (bf16[240,960]{1,0:T(8,128)(2,1)}, bf16[240,960]{1,0:T(8,128)(2,1)S(1)}, u32[]{:S(2)}, u32[]{:S(2)}) collective-permute-start(bf16[240,960]{1,0:T(8,128)(2,1)} %collective-permute-done.38.refs_21_), channel_id=1, source_target_pairs={{1,0},{5,4},{9,8},{13,12},{17,16},{21,20},{25,24},{29,28}} | collective-permute-start | bytes 1382408 | tf_op jit(solution)/shard_map/ppermute | solution.py:620
  173.5 32.2 %collective-permute-start.77 = (bf16[240,960]{1,0:T(8,128)(2,1)}, bf16[240,960]{1,0:T(8,128)(2,1)S(1)}, u32[]{:S(2)}, u32[]{:S(2)}) collective-permute-start(bf16[240,960]{1,0:T(8,128)(2,1)} %get-tuple-element.175), channel_id=1, source_target_pairs={{0,1},{1,0},{2,3},{3,2},{4,5},{5,4},{6,7},{7,6},{8,9},{9,8},{10,11... | collective-permute-start | bytes 1382408 | tf_op jit(solution)/shard_map/ppermute | solution.py:567
  175.6 27.5 %collective-permute-start.41 = (bf16[128,960]{1,0:T(8,128)(2,1)}, bf16[128,960]{1,0:T(8,128)(2,1)S(1)}, u32[]{:S(2)}, u32[]{:S(2)}) collective-permute-start(bf16[128,960]{1,0:T(8,128)(2,1)} %get-tuple-element.107), channel_id=1, source_target_pairs={{0,4},{4,0},{8,12},{12,8},{16,20},{20,16},{24,28},{28,24},{1,5},{5... | collective-permute-start | bytes 737288 | tf_op jit(solution)/shard_map/ppermute | solution.py:562
  179.4 24.1 %collective-permute-start.42 = (bf16[128,960]{1,0:T(8,128)(2,1)}, bf16[128,960]{1,0:T(8,128)(2,1)S(1)}, u32[]{:S(2)}, u32[]{:S(2)}) collective-permute-start(bf16[128,960]{1,0:T(8,128)(2,1)} %get-tuple-element.108), channel_id=1, source_target_pairs={{0,4},{4,0},{8,12},{12,8},{16,20},{20,16},{24,28},{28,24},{1,5},{5... | collective-permute-start | bytes 737288 | tf_op jit(solution)/shard_map/ppermute | solution.py:562
  185.7 25.3 %collective-permute-start.78 = (bf16[240,960]{1,0:T(8,128)(2,1)}, bf16[240,960]{1,0:T(8,128)(2,1)S(1)}, u32[]{:S(2)}, u32[]{:S(2)}) collective-permute-start(bf16[240,960]{1,0:T(8,128)(2,1)} %get-tuple-element.176), channel_id=1, source_target_pairs={{0,2},{1,3},{2,0},{3,1},{4,6},{5,7},{6,4},{7,5},{8,10},{9,11},{10,... | collective-permute-start | bytes 1382408 | tf_op jit(solution)/shard_map/ppermute | solution.py:567
  210.9 43.8 %collective-permute-start.79 = (bf16[240,960]{1,0:T(8,128)(2,1)}, bf16[240,960]{1,0:T(8,128)(2,1)}, u32[]{:S(2)}, u32[]{:S(2)}) collective-permute-start(bf16[240,960]{1,0:T(8,128)(2,1)} %get-tuple-element.177), channel_id=1, source_target_pairs={{0,3},{1,2},{2,1},{3,0},{4,7},{5,6},{6,5},{7,4},{8,11},{9,10},{10,... | collective-permute-start | bytes 1382408 | tf_op jit(solution)/shard_map/ppermute | solution.py:567
  213.7 33.4 %collective-permute-start.55 = (bf16[128,640]{1,0:T(8,128)(2,1)}, bf16[128,640]{1,0:T(8,128)(2,1)}, u32[]{:S(2)}, u32[]{:S(2)}) collective-permute-start(bf16[128,640]{1,0:T(8,128)(2,1)} %get-tuple-element.127), channel_id=1, source_target_pairs={{2,0},{3,1},{6,4},{7,5},{10,8},{11,9},{14,12},{15,13},{18,16},{19,... | collective-permute-start | bytes 491528 | tf_op jit(solution)/shard_map/ppermute | solution.py:573
  215.0 32.8 %collective-permute-start.56 = (bf16[128,640]{1,0:T(8,128)(2,1)}, bf16[128,640]{1,0:T(8,128)(2,1)}, u32[]{:S(2)}, u32[]{:S(2)}) collective-permute-start(bf16[128,640]{1,0:T(8,128)(2,1)} %get-tuple-element.128), channel_id=1, source_target_pairs={{3,0},{7,4},{11,8},{15,12},{19,16},{23,20},{27,24},{31,28}} | collective-permute-start | bytes 491528 | tf_op jit(solution)/shard_map/ppermute | solution.py:573
  219.2 35.6 %collective-permute-start.44 = (bf16[128,960]{1,0:T(8,128)(2,1)}, bf16[128,960]{1,0:T(8,128)(2,1)}, u32[]{:S(2)}, u32[]{:S(2)}) collective-permute-start(bf16[128,960]{1,0:T(8,128)(2,1)} %get-tuple-element.111), channel_id=1, source_target_pairs={{0,8},{4,12},{8,0},{12,4},{16,24},{20,28},{24,16},{28,20},{1,9},{5... | collective-permute-start | bytes 737288 | tf_op jit(solution)/shard_map/ppermute | solution.py:562
  229.4 41.3 %collective-permute-start.71 = (bf16[4,2,120,240]{3,2,1,0:T(8,128)(2,1)}, bf16[4,2,120,240]{3,2,1,0:T(8,128)(2,1)S(1)}, u32[]{:S(2)}, u32[]{:S(2)}) collective-permute-start(bf16[4,2,120,240]{3,2,1,0:T(8,128)(2,1)} %get-tuple-element.162), channel_id=1, source_target_pairs={{0,8},{4,12},{8,0},{12,4},{16,24},{20,28},{24,16},{28,20},{1,9},{5... | collective-permute-start | bytes 1382408 | tf_op jit(solution)/shard_map/ppermute | solution.py:562
  247.1 32.3 %collective-permute-start.72 = (bf16[4,2,120,240]{3,2,1,0:T(8,128)(2,1)}, bf16[4,2,120,240]{3,2,1,0:T(8,128)(2,1)S(1)}, u32[]{:S(2)}, u32[]{:S(2)}) collective-permute-start(bf16[4,2,120,240]{3,2,1,0:T(8,128)(2,1)} %get-tuple-element.163), channel_id=1, source_target_pairs={{0,16},{4,20},{8,24},{12,28},{16,0},{20,4},{24,8},{28,12},{1,17},{... | collective-permute-start | bytes 1382408 | tf_op jit(solution)/shard_map/ppermute | solution.py:562
  247.8 33.1 %collective-permute-start.73 = (bf16[4,2,120,240]{3,2,1,0:T(8,128)(2,1)}, bf16[4,2,120,240]{3,2,1,0:T(8,128)(2,1)}, u32[]{:S(2)}, u32[]{:S(2)}) collective-permute-start(bf16[4,2,120,240]{3,2,1,0:T(8,128)(2,1)} %get-tuple-element.164), channel_id=1, source_target_pairs={{0,24},{4,28},{8,16},{12,20},{16,8},{20,12},{24,0},{28,4},{1,25},{... | collective-permute-start | bytes 1382408 | tf_op jit(solution)/shard_map/ppermute | solution.py:562
  260.9 48.9 %all-to-all-start.1 = ((bf16[8,240,120]{2,1,0:T(8,128)(2,1)}), bf16[8,240,120]{2,1,0:T(8,128)(2,1)S(1)}, u32[]{:S(2)}, u32[]{:S(2)}) async-start(bf16[8,240,120]{2,1,0:T(8,128)(2,1)} %shard_map.225), calls=%async_computation.1 | async-start | bytes 983040 | tf_op jit(solution)/shard_map/all_to_all | solution.py:829
  264.5 34.2 %collective-permute-start.45 = (bf16[128,960]{1,0:T(8,128)(2,1)}, bf16[128,960]{1,0:T(8,128)(2,1)}, u32[]{:S(2)}, u32[]{:S(2)}) collective-permute-start(bf16[128,960]{1,0:T(8,128)(2,1)} %get-tuple-element.112), channel_id=1, source_target_pairs={{0,16},{4,20},{8,24},{12,28},{16,0},{20,4},{24,8},{28,12},{1,17},{... | collective-permute-start | bytes 737288 | tf_op jit(solution)/shard_map/ppermute | solution.py:562
  266.4 35.8 %collective-permute-start.46 = (bf16[128,960]{1,0:T(8,128)(2,1)}, bf16[128,960]{1,0:T(8,128)(2,1)}, u32[]{:S(2)}, u32[]{:S(2)}) collective-permute-start(bf16[128,960]{1,0:T(8,128)(2,1)} %get-tuple-element.113), channel_id=1, source_target_pairs={{0,24},{4,28},{8,16},{12,20},{16,8},{20,12},{24,0},{28,4},{1,25},{... | collective-permute-start | bytes 737288 | tf_op jit(solution)/shard_map/ppermute | solution.py:562
  284.5 29.7 %collective-permute-start.74 = (bf16[2,120,240]{2,1,0:T(8,128)(2,1)}, bf16[2,120,240]{2,1,0:T(8,128)(2,1)S(1)}, u32[]{:S(2)}, u32[]{:S(2)}) collective-permute-start(bf16[2,120,240]{2,1,0:T(8,128)(2,1)} %get-tuple-element.166), channel_id=1, source_target_pairs={{0,1},{1,0},{2,3},{3,2},{4,5},{5,4},{6,7},{7,6},{8,9},{9,8},{10,11... | collective-permute-start | bytes 345608 | tf_op jit(solution)/shard_map/ppermute | solution.py:567
  (110 other events, 1420.9 us)
where the time goes:
time: 317 us; the launch traced here: 316 us
  waiting for transfers between devices  130 us (41%)
  Pallas kernels  92.8 us (29%)
  starting transfers between devices  80.2 us (25%)
  local copies, waits for them, and re-layouts  10.5 us (3%)
    pallas_call x24, Pallas kernels, call(): pl.pallas_call(kernel, out_shape=outs, in_specs=[free if i < far else vme...  92.8 us
    ppermute x56, waiting for transfers between devices, flip(): return lax.ppermute(x, 'batch', [(i, i ^ bits) for i in range(n)])  70.1 us
    ppermute x56, starting transfers between devices, flip(): return lax.ppermute(x, 'batch', [(i, i ^ bits) for i in range(n)])  33.5 us
    ppermute x6, waiting for transfers between devices, push(): return lax.ppermute(x, 'seq', pairs)  22.7 us
    ppermute x12, waiting for transfers between devices, cross(): return lax.ppermute(x, 'seq', [(i, i ^ bits) for i in range(n)])  21.7 us
    ppermute x6, waiting for transfers between devices, step(): return lax.ppermute(x, 'seq', [(i, i + by) for i in senders])  15.5 us
    ppermute x12, starting transfers between devices, cross(): return lax.ppermute(x, 'seq', [(i, i ^ bits) for i in range(n)])  14.8 us
    ppermute x6, starting transfers between devices, push(): return lax.ppermute(x, 'seq', pairs)  13.4 us
  transfers between devices with their start and end apart: 82, of which 26 were waited for; matrix products, arithmetic and copies ran while one was open for 0% of the time, Pallas kernels for 24%

commit v1 on v0

--- a/solution.py
+++ b/solution.py
@@ -533,13 +533,14 @@
     return math.prod(outer) * (-(-rows // tile) * tile) * (-(-lanes // 128) * 128) * size
 
 
-def call(kernel, outs, scratch, flops, *args, far=0, far_outs=(), room=None):
+def call(kernel, outs, scratch, flops, *args, far=0, far_outs=()):
     sizes = [a.size * a.dtype.itemsize for a in (*args, *outs)]
     vmem = pl.BlockSpec(memory_space=pltpu.VMEM)
     free = pl.BlockSpec(memory_space=pl.ANY)
-    limit = None
-    if room is not None:
-        limit = sum(padded(a) for a in (*args, *outs)) + room * 2**20
+    held = [a for i, a in enumerate(args) if i >= far]
+    held += [a for i, a in enumerate(outs) if i not in far_outs]
+    held += [array(*x) for x in scratch if isinstance(x, tuple)]
+    limit = min(sum(padded(a) for a in held) + ROOM * 2**20, 60 * 1024 * 2**10)
     return pl.pallas_call(
         kernel,
         out_shape=outs,
@@ -669,7 +670,6 @@
         1e5,
         own,
         *[cross(own, k) for k in others],
-        room=ROOM,
     )
     kv_near = plane_hops(kv_slots, chips)
     kv_far = pair_swap(kv_near)
@@ -686,7 +686,7 @@
         down_weight.T,
     )
     spread = lax.all_to_all(local, "batch", split_axis=0, concat_axis=0, tiled=True)
-    (feed_own,) = call(arrange_kernel, [array((3 * units, width), BF)], [], 1e5, spread, room=ROOM)
+    (feed_own,) = call(arrange_kernel, [array((3 * units, width), BF)], [], 1e5, spread)
     feed_right, feed_left = line_chain(feed_own, line)
 
     (low,) = call(cast_kernel, [array((piece, width), BF)], [], 1e5, grad_rows)
@@ -813,18 +813,12 @@
 
     down_own, down_got = plane_sum(down_near, down_far, chips)
     (block_output,) = call(
-        down_end_kernel, [array((width, piece), F32)], [], 1e6, mid, down_own, *down_got, room=ROOM
+        down_end_kernel, [array((width, piece), F32)], [], 1e6, mid, down_own, *down_got
     )
 
     feed_got = [cross(feed_grads[k], k) for k in others]
     (feed_own,) = call(
-        feed_end_kernel,
-        [array((size, 3 * units, cut), BF)],
-        [],
-        1e6,
-        feed_grads[0],
-        *feed_got,
-        room=ROOM,
+        feed_end_kernel, [array((size, 3 * units, cut), BF)], [], 1e6, feed_grads[0], *feed_got
     )
     feed_back = lax.all_to_all(feed_own, "batch", split_axis=0, concat_axis=0, tiled=True)
     gate_done, up_done, down_done = call(
@@ -837,7 +831,6 @@
         [],
         1e6,
         feed_back.reshape(size, 3, units, cut),
-        room=ROOM,
     )
 
     shape = (line, 2, cut, qo_cols)
@@ -862,11 +855,10 @@
         1e6,
         qo_own,
         *qo_got,
-        room=ROOM,
     )
     qo_got = [cross(qo_sent[k - 1], k) for k in others]
     query_done, output_done = call(
-        qo_end_kernel, [array((cut, qo_cols), F32)] * 2, [], 1e6, qo_own, *qo_got, room=ROOM
+        qo_end_kernel, [array((cut, qo_cols), F32)] * 2, [], 1e6, qo_own, *qo_got
     )
 
     each = width // kv_cols
@@ -904,7 +896,6 @@
         1e6,
         kv_own,
         *kv_got,
-        room=ROOM,
     )
     kv_got = [cross(kv_sent[k - 1], k) for k in others]
     key_done, value_done, attn_gain_sum, feed_gain_sum = call(
@@ -915,7 +906,6 @@
         kv_own,
         own_gains,
         *kv_got,
-        room=ROOM,
     )
     return (
         block_output.T[None],

time: 317 us -> 294 us (0.927)
  Pallas kernels: 92.8 us -> 48.5 us
  local copies, waits for them, and re-layouts: 10.5 us -> 28 us
    pallas_call x24, Pallas kernels: 92.8 us -> 48.5 us  [call(): pl.pallas_call(kernel, out_shape=outs, in_specs=[free if i < far else vme...]
    unnamed x104 -> x122, local copies, waits for them, and re-layouts: 10.5 us -> 28 us
    ppermute x56, waiting for transfers between devices: 70.1 us -> 55.5 us  [flip(): return lax.ppermute(x, 'batch', [(i, i ^ bits) for i in range(n)])]
    ppermute x12, waiting for transfers between devices: 21.7 us -> 33 us  [cross(): return lax.ppermute(x, 'seq', [(i, i ^ bits) for i in range(n)])]
    ppermute x6, waiting for transfers between devices: 22.7 us -> 26.8 us  [push(): return lax.ppermute(x, 'seq', pairs)]
  transfers between devices with their start and end apart: 82 -> 82, of which waited for: 26 -> 25; matrix products, arithmetic and copies ran while one was open for 0% -> 0% of each run, Pallas kernels for 24% -> 13%
where the time goes in v1:
time: 294 us; the launch traced here: 292 us
  waiting for transfers between devices  133 us (45%)
  starting transfers between devices  80.8 us (27%)
  Pallas kernels  48.5 us (16%)
  local copies, waits for them, and re-layouts  28 us (10%)
    ppermute x56, waiting for transfers between devices, flip(): return lax.ppermute(x, 'batch', [(i, i ^ bits) for i in range(n)])  55.5 us
    pallas_call x24, Pallas kernels, call(): pl.pallas_call(kernel, out_shape=outs, in_specs=[free if i < far else vme...  48.5 us
    ppermute x12, waiting for transfers between devices, cross(): return lax.ppermute(x, 'seq', [(i, i ^ bits) for i in range(n)])  33 us
    ppermute x56, starting transfers between devices, flip(): return lax.ppermute(x, 'batch', [(i, i ^ bits) for i in range(n)])  32.6 us
    unnamed x122, local copies, waits for them, and re-layouts  28 us
    ppermute x6, waiting for transfers between devices, push(): return lax.ppermute(x, 'seq', pairs)  26.8 us
    ppermute x6, waiting for transfers between devices, step(): return lax.ppermute(x, 'seq', [(i, i + by) for i in senders])  18.2 us
    ppermute x12, starting transfers between devices, cross(): return lax.ppermute(x, 'seq', [(i, i ^ bits) for i in range(n)])  17.2 us
  transfers between devices with their start and end apart: 82, of which 25 were waited for; matrix products, arithmetic and copies ran while one was open for 0% of the time, Pallas kernels for 13%

profile of v1, /device:TPU:0, one launch (start us, length us, event | category | flops | bytes accessed | tf_op | source)
XLA Modules:
  0.0 292.4 jit_solution(4333573880407550126)
XLA Ops:
  4.0 5.1 %collective-permute-start.2 = (bf16[120,640]{1,0:T(8,128)(2,1)S(1)}, bf16[120,640]{1,0:T(8,128)(2,1)S(1)}, u32[]{:S(2)}, u32[]{:S(2)}) collective-permute-start(bf16[120,640]{1,0:T(8,128)(2,1)S(1)} %shard_map.203.refs_0_), channel_id=1, source_target_pairs={{0,3},{1,2},{2,1},{3,0},{4,7},{5,6},{6,5},{7,4},{8,11},{9,10},{10,... | collective-permute-start | bytes 460808 | tf_op jit(solution)/shard_map/ppermute | solution.py:568
  14.1 8.1 %collective-permute-done.1.refs_2_ = bf16[120,640]{1,0:T(8,128)(2,1)S(1)} collective-permute-done((bf16[120,640]{1,0:T(8,128)(2,1)S(1)}, bf16[120,640]{1,0:T(8,128)(2,1)S(1)}, u32[]{:S(2)}, u32[]{:S(2)}) %collective-permute-start.1) | collective-permute-done | bytes 153632 | tf_op jit(solution)/shard_map/ppermute | solution.py:568
  26.0 6.3 %collective-permute-done.5.refs_8_.refs_15_ = bf16[4,120,160]{2,1,0:T(8,128)(2,1)S(1)} collective-permute-done((bf16[4,120,160]{2,1,0:T(8,128)(2,1)S(1)}, bf16[4,120,160]{2,1,0:T(8,128)(2,1)S(1)}, u32[]{:S(2)}, u32[]{:S(2)}) %collective-permute-start.5) | collective-permute-done | bytes 153632 | tf_op jit(solution)/shard_map/ppermute | solution.py:563
  40.7 4.1 %all-to-all-start = ((bf16[8,3,80,120]{3,2,1,0:T(8,128)(2,1)}), bf16[8,3,80,120]{3,2,1,0:T(8,128)(2,1)}, u32[]{:S(2)}, u32[]{:S(2)}) async-start(bf16[8,3,80,120]{3,2,1,0:T(8,128)(2,1)} %shard_map.209), calls=%async_computation | async-start | bytes 983040 | tf_op jit(solution)/shard_map/all_to_all | solution.py:688
  65.6 5.4 %collective-permute-done.29.refs_11_ = bf16[128,960]{1,0:T(8,128)(2,1)} collective-permute-done((bf16[128,960]{1,0:T(8,128)(2,1)}, bf16[128,960]{1,0:T(8,128)(2,1)}, u32[]{:S(2)}, u32[]{:S(2)}) %collective-permute-start.29) | collective-permute-done | bytes 245792 | tf_op jit(solution)/shard_map/ppermute | solution.py:563
  70.9 4.9 %collective-permute-start.19 = (bf16[136,640]{1,0:T(8,128)(2,1)S(1)}, bf16[136,640]{1,0:T(8,128)(2,1)}, u32[]{:S(2)}, u32[]{:S(2)}) collective-permute-start(bf16[136,640]{1,0:T(8,128)(2,1)S(1)} %get-tuple-element.99.refs_1_.refs_20_), channel_id=1, source_target_pairs={{0,3},{4,7},{8,11},{12,15},{16,19},{20,23},{24,27},{28,31}} | collective-permute-start | bytes 522248 | tf_op jit(solution)/shard_map/ppermute | solution.py:574
  82.9 4.6 %collective-permute-start.34 = (bf16[240,960]{1,0:T(8,128)(2,1)S(1)}, bf16[240,960]{1,0:T(8,128)(2,1)S(1)}, u32[]{:S(2)}, u32[]{:S(2)}) collective-permute-start(bf16[240,960]{1,0:T(8,128)(2,1)S(1)} %shard_map.210.refs_16_), channel_id=1, source_target_pairs={{0,1},{1,2},{2,3},{4,5},{5,6},{6,7},{8,9},{9,10},{10,11},{12,13},{... | collective-permute-start | bytes 1382408 | tf_op jit(solution)/shard_map/ppermute | solution.py:621
  88.2 7.8 %collective-permute-done.37.refs_20_ = bf16[240,960]{1,0:T(8,128)(2,1)S(1)} collective-permute-done((bf16[240,960]{1,0:T(8,128)(2,1)S(1)}, bf16[240,960]{1,0:T(8,128)(2,1)S(1)}, u32[]{:S(2)}, u32[]{:S(2)}) %collective-permute-start.37) | collective-permute-done | bytes 460832 | tf_op jit(solution)/shard_map/ppermute | solution.py:621
  101.2 5.5 %shard_map.207 = (f32[5,384,512]{2,1,0:T(8,128)S(1)}, bf16[128,960]{1,0:T(8,128)(2,1)S(1)}, f32[128,960]{1,0:T(8,128)S(1)}, bf16[128,960]{1,0:T(8,128)(2,1)S(1)}) custom-call(bf16[128,960]{1,0:T(8,128)(2,1)S(1)} %shard_map.206.refs_0_.refs_8_, bf16[136,640]{1,0:T(8,128)(2,1)S(1)} %get-tuple-element.99.refs_1_.refs_20_, ...), custom_call_target="tpu_custom_call" | custom-call | flops 487587840 | bytes 10039552 | tf_op jit(solution)/shard_map/pallas_call | solution.py:544
  118.6 5.0 %collective-permute-done.21.refs_2_ = bf16[128,960]{1,0:T(8,128)(2,1)S(1)} collective-permute-done((bf16[128,960]{1,0:T(8,128)(2,1)S(1)}, bf16[128,960]{1,0:T(8,128)(2,1)S(1)}, u32[]{:S(2)}, u32[]{:S(2)}) %collective-permute-start.21) | collective-permute-done | bytes 245792 | tf_op jit(solution)/shard_map/ppermute | solution.py:563
  125.5 6.3 %collective-permute-done.39.refs_22_ = bf16[240,960]{1,0:T(8,128)(2,1)S(1)} collective-permute-done((bf16[240,960]{1,0:T(8,128)(2,1)S(1)}, bf16[240,960]{1,0:T(8,128)(2,1)S(1)}, u32[]{:S(2)}, u32[]{:S(2)}) %collective-permute-start.39) | collective-permute-done | bytes 460832 | tf_op jit(solution)/shard_map/ppermute | solution.py:621
  131.8 8.9 %shard_map.211 = (bf16[512,960]{1,0:T(8,128)(2,1)S(1)}, bf16[128,960]{1,0:T(8,128)(2,1)S(1)}, bf16[128,960]{1,0:T(8,128)(2,1)S(1)}, bf16[128,960]{1,0:T(8,128)(2...) custom-call(bf16[128,960]{1,0:T(8,128)(2,1)S(1)} %get-tuple-element., ...), custom_call_target="tpu_custom_call" | custom-call | flops 3145728000 | bytes 11089920 | tf_op jit(solution)/shard_map/pallas_call | solution.py:544
  141.8 5.3 %shard_map.212 = (bf16[512,960]{1,0:T(8,128)(2,1)S(1)}, bf16[128,960]{1,0:T(8,128)(2,1)S(1)}, bf16[128,960]{1,0:T(8,128)(2,1)S(1)}, bf16[128,960]{1,0:T(8,128)(2...) custom-call(bf16[128,960]{1,0:T(8,128)(2,1)S(1)} %get-tuple-element., ...), custom_call_target="tpu_custom_call" | custom-call | flops 2516582400 | bytes 13393920 | tf_op jit(solution)/shard_map/pallas_call | solution.py:544
  152.6 4.2 %collective-permute-done.51.refs_1_ = bf16[128,960]{1,0:T(8,128)(2,1)S(1)} collective-permute-done((bf16[128,960]{1,0:T(8,128)(2,1)S(1)}, bf16[128,960]{1,0:T(8,128)(2,1)S(1)}, u32[]{:S(2)}, u32[]{:S(2)}) %collective-permute-start.51) | collective-permute-done | bytes 245792 | tf_op jit(solution)/shard_map/ppermute | solution.py:563
  156.8 6.3 %collective-permute-done.52.refs_2_ = bf16[128,960]{1,0:T(8,128)(2,1)S(1)} collective-permute-done((bf16[128,960]{1,0:T(8,128)(2,1)S(1)}, bf16[128,960]{1,0:T(8,128)(2,1)S(1)}, u32[]{:S(2)}, u32[]{:S(2)}) %collective-permute-start.52) | collective-permute-done | bytes 245792 | tf_op jit(solution)/shard_map/ppermute | solution.py:563
  164.4 6.4 %shard_map.216 = (f32[128,960]{1,0:T(8,128)S(1)}, f32[1,960]{1,0:T(1,128)S(1)}, bf16[128,960]{1,0:T(8,128)(2,1)S(1)}, bf16[128,960]{1,0:T(8,128)(2,1)S(1)}, f32[...) custom-call(f32[128,960]{1,0:T(8,128)S(1)} %get-tuple-element.119.re, ...), custom_call_target="tpu_custom_call" | custom-call | flops 739246080 | bytes 12860928 | tf_op jit(solution)/shard_map/pallas_call | solution.py:544
  174.4 13.8 %collective-permute-done.78.refs_1_ = bf16[240,960]{1,0:T(8,128)(2,1)S(1)} collective-permute-done((bf16[240,960]{1,0:T(8,128)(2,1)S(1)}, bf16[240,960]{1,0:T(8,128)(2,1)S(1)}, u32[]{:S(2)}, u32[]{:S(2)}) %collective-permute-start.78) | collective-permute-done | bytes 460832 | tf_op jit(solution)/shard_map/ppermute | solution.py:568
  197.4 8.9 %collective-permute-done.54.refs_1_ = bf16[128,640]{1,0:T(8,128)(2,1)S(1)} collective-permute-done((bf16[128,640]{1,0:T(8,128)(2,1)S(1)}, bf16[128,640]{1,0:T(8,128)(2,1)S(1)}, u32[]{:S(2)}, u32[]{:S(2)}) %collective-permute-start.54) | collective-permute-done | bytes 163872 | tf_op jit(solution)/shard_map/ppermute | solution.py:574
  206.9 17.8 %collective-permute-done.55.refs_2_ = bf16[128,640]{1,0:T(8,128)(2,1)S(1)} collective-permute-done((bf16[128,640]{1,0:T(8,128)(2,1)S(1)}, bf16[128,640]{1,0:T(8,128)(2,1)S(1)}, u32[]{:S(2)}, u32[]{:S(2)}) %collective-permute-start.55) | collective-permute-done | bytes 163872 | tf_op jit(solution)/shard_map/ppermute | solution.py:574
  237.0 3.6 %all-to-all-start.1 = ((bf16[8,240,120]{2,1,0:T(8,128)(2,1)}), bf16[8,240,120]{2,1,0:T(8,128)(2,1)S(1)}, u32[]{:S(2)}, u32[]{:S(2)}) async-start(bf16[8,240,120]{2,1,0:T(8,128)(2,1)} %shard_map.225), calls=%async_computation.1 | async-start | bytes 983040 | tf_op jit(solution)/shard_map/all_to_all | solution.py:823
  248.5 8.9 %collective-permute-done.72.refs_1_ = bf16[4,2,120,240]{3,2,1,0:T(8,128)(2,1)} collective-permute-done((bf16[4,2,120,240]{3,2,1,0:T(8,128)(2,1)}, bf16[4,2,120,240]{3,2,1,0:T(8,128)(2,1)}, u32[]{:S(2)}, u32[]{:S(2)}) %collective-permute-start.72) | collective-permute-done | bytes 460832 | tf_op jit(solution)/shard_map/ppermute | solution.py:563
  262.8 12.3 %collective-permute-done.62.refs_1_ = bf16[496,160]{1,0:T(8,128)(2,1)S(1)} collective-permute-done((bf16[496,160]{1,0:T(8,128)(2,1)S(1)}, bf16[496,160]{1,0:T(8,128)(2,1)S(1)}, u32[]{:S(2)}, u32[]{:S(2)}) %collective-permute-start.62) | collective-permute-done | bytes 158752 | tf_op jit(solution)/shard_map/ppermute | solution.py:563
  279.8 4.4 %collective-permute-done.64.refs_0_ = bf16[136,160]{1,0:T(8,128)(2,1)S(1)} collective-permute-done((bf16[136,160]{1,0:T(8,128)(2,1)S(1)}, bf16[136,160]{1,0:T(8,128)(2,1)S(1)}, u32[]{:S(2)}, u32[]{:S(2)}) %collective-permute-start.64) | collective-permute-done | bytes 43552 | tf_op jit(solution)/shard_map/ppermute | solution.py:568
  286.5 4.3 %collective-permute-done.65.refs_1_ = bf16[136,160]{1,0:T(8,128)(2,1)S(1)} collective-permute-done((bf16[136,160]{1,0:T(8,128)(2,1)S(1)}, bf16[136,160]{1,0:T(8,128)(2,1)S(1)}, u32[]{:S(2)}, u32[]{:S(2)}) %collective-permute-start.65) | collective-permute-done | bytes 43552 | tf_op jit(solution)/shard_map/ppermute | solution.py:568
  (289 shorter events, 122.8 us)
Async XLA Ops:
  11.7 33.2 %collective-permute-start.30 = (bf16[128,960]{1,0:T(8,128)(2,1)}, bf16[128,960]{1,0:T(8,128)(2,1)S(1)}, u32[]{:S(2)}, u32[]{:S(2)}) collective-permute-start(bf16[128,960]{1,0:T(8,128)(2,1)} %shard_map.208.refs_8_), channel_id=1, source_target_pairs={{0,4},{4,0},{8,12},{12,8},{16,20},{20,16},{24,28},{28,24},{1,5},{5... | collective-permute-start | bytes 737288 | tf_op jit(solution)/shard_map/ppermute | solution.py:563
  26.0 20.0 %collective-permute-start.6 = (bf16[4,120,160]{2,1,0:T(8,128)(2,1)S(1)}, bf16[4,120,160]{2,1,0:T(8,128)(2,1)S(1)}, u32[]{:S(2)}, u32[]{:S(2)}) collective-permute-start(bf16[4,120,160]{2,1,0:T(8,128)(2,1)S(1)} %get-tuple-element.96.refs_5_.refs_12_), channel_id=1, source_target_pairs={{0,4},{4,0},{8,12},{12,8},{16,20},{20,16},{24,28},{28,24},{1,5},{5... | collective-permute-start | bytes 460808 | tf_op jit(solution)/shard_map/ppermute | solution.py:563
  40.7 39.6 %all-to-all-start = ((bf16[8,3,80,120]{3,2,1,0:T(8,128)(2,1)}), bf16[8,3,80,120]{3,2,1,0:T(8,128)(2,1)}, u32[]{:S(2)}, u32[]{:S(2)}) async-start(bf16[8,3,80,120]{3,2,1,0:T(8,128)(2,1)} %shard_map.209), calls=%async_computation | async-start | bytes 983040 | tf_op jit(solution)/shard_map/all_to_all | solution.py:688
  45.6 30.2 %collective-permute-start.13 = (bf16[4,2,120,240]{3,2,1,0:T(8,128)(2,1)S(1)}, bf16[4,2,120,240]{3,2,1,0:T(8,128)(2,1)S(1)}, u32[]{:S(2)}, u32[]{:S(2)}) collective-permute-start(bf16[4,2,120,240]{3,2,1,0:T(8,128)(2,1)S(1)} %get-tuple-element.98.refs_3_.refs_8_.refs_12_.refs_4_), channel_id=1, source_target_pairs={{0,4},{4,0},{8,12},{12,8},{16,20},{20,16},{24,28},{28,24},{1,5},{5... | collective-permute-start | bytes 1382408 | tf_op jit(solution)/shard_map/ppermute | solution.py:563
  46.7 31.1 %collective-permute-start.12 = (bf16[4,2,120,240]{3,2,1,0:T(8,128)(2,1)S(1)}, bf16[4,2,120,240]{3,2,1,0:T(8,128)(2,1)S(1)}, u32[]{:S(2)}, u32[]{:S(2)}) collective-permute-start(bf16[4,2,120,240]{3,2,1,0:T(8,128)(2,1)S(1)} %get-tuple-element.98.refs_3_.refs_8_.refs_12_.refs_4_), channel_id=1, source_target_pairs={{0,24},{4,28},{8,16},{12,20},{16,8},{20,12},{24,0},{28,4},{1,25},{... | collective-permute-start | bytes 1382408 | tf_op jit(solution)/shard_map/ppermute | solution.py:563
  49.9 21.0 %collective-permute-start.29 = (bf16[128,960]{1,0:T(8,128)(2,1)}, bf16[128,960]{1,0:T(8,128)(2,1)}, u32[]{:S(2)}, u32[]{:S(2)}) collective-permute-start(bf16[128,960]{1,0:T(8,128)(2,1)} %shard_map.208.refs_8_), channel_id=1, source_target_pairs={{0,24},{4,28},{8,16},{12,20},{16,8},{20,12},{24,0},{28,4},{1,25},{... | collective-permute-start | bytes 737288 | tf_op jit(solution)/shard_map/ppermute | solution.py:563
  51.0 30.6 %collective-permute-start.11 = (bf16[4,2,120,240]{3,2,1,0:T(8,128)(2,1)S(1)}, bf16[4,2,120,240]{3,2,1,0:T(8,128)(2,1)S(1)}, u32[]{:S(2)}, u32[]{:S(2)}) collective-permute-start(bf16[4,2,120,240]{3,2,1,0:T(8,128)(2,1)S(1)} %get-tuple-element.98.refs_3_.refs_8_.refs_12_.refs_4_), channel_id=1, source_target_pairs={{0,16},{4,20},{8,24},{12,28},{16,0},{20,4},{24,8},{28,12},{1,17},{... | collective-permute-start | bytes 1382408 | tf_op jit(solution)/shard_map/ppermute | solution.py:563
  53.4 29.5 %collective-permute-start.10 = (bf16[4,2,120,240]{3,2,1,0:T(8,128)(2,1)S(1)}, bf16[4,2,120,240]{3,2,1,0:T(8,128)(2,1)S(1)}, u32[]{:S(2)}, u32[]{:S(2)}) collective-permute-start(bf16[4,2,120,240]{3,2,1,0:T(8,128)(2,1)S(1)} %get-tuple-element.98.refs_3_.refs_8_.refs_12_.refs_4_), channel_id=1, source_target_pairs={{0,8},{4,12},{8,0},{12,4},{16,24},{20,28},{24,16},{28,20},{1,9},{5... | collective-permute-start | bytes 1382408 | tf_op jit(solution)/shard_map/ppermute | solution.py:563
  151.1 23.0 %collective-permute-start.77 = (bf16[240,960]{1,0:T(8,128)(2,1)S(1)}, bf16[240,960]{1,0:T(8,128)(2,1)S(1)}, u32[]{:S(2)}, u32[]{:S(2)}) collective-permute-start(bf16[240,960]{1,0:T(8,128)(2,1)S(1)} %get-tuple-element.175), channel_id=1, source_target_pairs={{0,1},{1,0},{2,3},{3,2},{4,5},{5,4},{6,7},{7,6},{8,9},{9,8},{10,11... | collective-permute-start | bytes 1382408 | tf_op jit(solution)/shard_map/ppermute | solution.py:568
  152.6 20.7 %collective-permute-start.41 = (bf16[128,960]{1,0:T(8,128)(2,1)S(1)}, bf16[128,960]{1,0:T(8,128)(2,1)S(1)}, u32[]{:S(2)}, u32[]{:S(2)}) collective-permute-start(bf16[128,960]{1,0:T(8,128)(2,1)S(1)} %get-tuple-element.107), channel_id=1, source_target_pairs={{0,4},{4,0},{8,12},{12,8},{16,20},{20,16},{24,28},{28,24},{1,5},{5... | collective-permute-start | bytes 737288 | tf_op jit(solution)/shard_map/ppermute | solution.py:563
  163.1 25.1 %collective-permute-start.78 = (bf16[240,960]{1,0:T(8,128)(2,1)S(1)}, bf16[240,960]{1,0:T(8,128)(2,1)S(1)}, u32[]{:S(2)}, u32[]{:S(2)}) collective-permute-start(bf16[240,960]{1,0:T(8,128)(2,1)S(1)} %get-tuple-element.176), channel_id=1, source_target_pairs={{0,2},{1,3},{2,0},{3,1},{4,6},{5,7},{6,4},{7,5},{8,10},{9,11},{10,... | collective-permute-start | bytes 1382408 | tf_op jit(solution)/shard_map/ppermute | solution.py:568
  173.9 19.1 %collective-permute-start.69 = (bf16[4,2,120,240]{3,2,1,0:T(8,128)(2,1)S(1)}, bf16[4,2,120,240]{3,2,1,0:T(8,128)(2,1)S(1)}, u32[]{:S(2)}, u32[]{:S(2)}) collective-permute-start(bf16[4,2,120,240]{3,2,1,0:T(8,128)(2,1)S(1)} %get-tuple-element.159), channel_id=1, source_target_pairs={{0,4},{4,0},{8,12},{12,8},{16,20},{20,16},{24,28},{28,24},{1,5},{5... | collective-permute-start | bytes 1382408 | tf_op jit(solution)/shard_map/ppermute | solution.py:563
  174.1 21.5 %collective-permute-start.70 = (bf16[4,2,120,240]{3,2,1,0:T(8,128)(2,1)S(1)}, bf16[4,2,120,240]{3,2,1,0:T(8,128)(2,1)S(1)}, u32[]{:S(2)}, u32[]{:S(2)}) collective-permute-start(bf16[4,2,120,240]{3,2,1,0:T(8,128)(2,1)S(1)} %get-tuple-element.160), channel_id=1, source_target_pairs={{0,4},{4,0},{8,12},{12,8},{16,20},{20,16},{24,28},{28,24},{1,5},{5... | collective-permute-start | bytes 1382408 | tf_op jit(solution)/shard_map/ppermute | solution.py:563
  188.2 44.1 %collective-permute-start.79 = (bf16[240,960]{1,0:T(8,128)(2,1)S(1)}, bf16[240,960]{1,0:T(8,128)(2,1)S(1)}, u32[]{:S(2)}, u32[]{:S(2)}) collective-permute-start(bf16[240,960]{1,0:T(8,128)(2,1)S(1)} %get-tuple-element.177), channel_id=1, source_target_pairs={{0,3},{1,2},{2,1},{3,0},{4,7},{5,6},{6,5},{7,4},{8,11},{9,10},{10,... | collective-permute-start | bytes 1382408 | tf_op jit(solution)/shard_map/ppermute | solution.py:568
  191.6 33.1 %collective-permute-start.55 = (bf16[128,640]{1,0:T(8,128)(2,1)S(1)}, bf16[128,640]{1,0:T(8,128)(2,1)S(1)}, u32[]{:S(2)}, u32[]{:S(2)}) collective-permute-start(bf16[128,640]{1,0:T(8,128)(2,1)S(1)} %get-tuple-element.127), channel_id=1, source_target_pairs={{2,0},{3,1},{6,4},{7,5},{10,8},{11,9},{14,12},{15,13},{18,16},{19,... | collective-permute-start | bytes 491528 | tf_op jit(solution)/shard_map/ppermute | solution.py:574
  193.0 32.3 %collective-permute-start.56 = (bf16[128,640]{1,0:T(8,128)(2,1)S(1)}, bf16[128,640]{1,0:T(8,128)(2,1)S(1)}, u32[]{:S(2)}, u32[]{:S(2)}) collective-permute-start(bf16[128,640]{1,0:T(8,128)(2,1)S(1)} %get-tuple-element.128), channel_id=1, source_target_pairs={{3,0},{7,4},{11,8},{15,12},{19,16},{23,20},{27,24},{31,28}} | collective-permute-start | bytes 491528 | tf_op jit(solution)/shard_map/ppermute | solution.py:574
  195.6 36.8 %collective-permute-start.44 = (bf16[128,960]{1,0:T(8,128)(2,1)S(1)}, bf16[128,960]{1,0:T(8,128)(2,1)S(1)}, u32[]{:S(2)}, u32[]{:S(2)}) collective-permute-start(bf16[128,960]{1,0:T(8,128)(2,1)S(1)} %get-tuple-element.111), channel_id=1, source_target_pairs={{0,8},{4,12},{8,0},{12,4},{16,24},{20,28},{24,16},{28,20},{1,9},{5... | collective-permute-start | bytes 737288 | tf_op jit(solution)/shard_map/ppermute | solution.py:563
  206.4 41.9 %collective-permute-start.71 = (bf16[4,2,120,240]{3,2,1,0:T(8,128)(2,1)}, bf16[4,2,120,240]{3,2,1,0:T(8,128)(2,1)}, u32[]{:S(2)}, u32[]{:S(2)}) collective-permute-start(bf16[4,2,120,240]{3,2,1,0:T(8,128)(2,1)} %get-tuple-element.162), channel_id=1, source_target_pairs={{0,8},{4,12},{8,0},{12,4},{16,24},{20,28},{24,16},{28,20},{1,9},{5... | collective-permute-start | bytes 1382408 | tf_op jit(solution)/shard_map/ppermute | solution.py:563
  224.7 32.7 %collective-permute-start.72 = (bf16[4,2,120,240]{3,2,1,0:T(8,128)(2,1)}, bf16[4,2,120,240]{3,2,1,0:T(8,128)(2,1)}, u32[]{:S(2)}, u32[]{:S(2)}) collective-permute-start(bf16[4,2,120,240]{3,2,1,0:T(8,128)(2,1)} %get-tuple-element.163), channel_id=1, source_target_pairs={{0,16},{4,20},{8,24},{12,28},{16,0},{20,4},{24,8},{28,12},{1,17},{... | collective-permute-start | bytes 1382408 | tf_op jit(solution)/shard_map/ppermute | solution.py:563
  225.3 33.2 %collective-permute-start.73 = (bf16[4,2,120,240]{3,2,1,0:T(8,128)(2,1)}, bf16[4,2,120,240]{3,2,1,0:T(8,128)(2,1)}, u32[]{:S(2)}, u32[]{:S(2)}) collective-permute-start(bf16[4,2,120,240]{3,2,1,0:T(8,128)(2,1)} %get-tuple-element.164), channel_id=1, source_target_pairs={{0,24},{4,28},{8,16},{12,20},{16,8},{20,12},{24,0},{28,4},{1,25},{... | collective-permute-start | bytes 1382408 | tf_op jit(solution)/shard_map/ppermute | solution.py:563
  237.0 48.2 %all-to-all-start.1 = ((bf16[8,240,120]{2,1,0:T(8,128)(2,1)}), bf16[8,240,120]{2,1,0:T(8,128)(2,1)S(1)}, u32[]{:S(2)}, u32[]{:S(2)}) async-start(bf16[8,240,120]{2,1,0:T(8,128)(2,1)} %shard_map.225), calls=%async_computation.1 | async-start | bytes 983040 | tf_op jit(solution)/shard_map/all_to_all | solution.py:823
  240.7 34.7 %collective-permute-start.45 = (bf16[128,960]{1,0:T(8,128)(2,1)}, bf16[128,960]{1,0:T(8,128)(2,1)S(1)}, u32[]{:S(2)}, u32[]{:S(2)}) collective-permute-start(bf16[128,960]{1,0:T(8,128)(2,1)} %copy-done.60), channel_id=1, source_target_pairs={{0,16},{4,20},{8,24},{12,28},{16,0},{20,4},{24,8},{28,12},{1,17},{... | collective-permute-start | bytes 737288 | tf_op jit(solution)/shard_map/ppermute | solution.py:563
  242.6 36.3 %collective-permute-start.46 = (bf16[128,960]{1,0:T(8,128)(2,1)}, bf16[128,960]{1,0:T(8,128)(2,1)S(1)}, u32[]{:S(2)}, u32[]{:S(2)}) collective-permute-start(bf16[128,960]{1,0:T(8,128)(2,1)} %copy-done.59), channel_id=1, source_target_pairs={{0,24},{4,28},{8,16},{12,20},{16,8},{20,12},{24,0},{28,4},{1,25},{... | collective-permute-start | bytes 737288 | tf_op jit(solution)/shard_map/ppermute | solution.py:563
  260.7 31.0 %collective-permute-start.74 = (bf16[2,120,240]{2,1,0:T(8,128)(2,1)S(1)}, bf16[2,120,240]{2,1,0:T(8,128)(2,1)S(1)}, u32[]{:S(2)}, u32[]{:S(2)}) collective-permute-start(bf16[2,120,240]{2,1,0:T(8,128)(2,1)S(1)} %get-tuple-element.166), channel_id=1, source_target_pairs={{0,1},{1,0},{2,3},{3,2},{4,5},{5,4},{6,7},{7,6},{8,9},{9,8},{10,11... | collective-permute-start | bytes 345608 | tf_op jit(solution)/shard_map/ppermute | solution.py:568
  (119 other events, 1715.9 us)

commit v2 on v1

--- a/solution.py
+++ b/solution.py
@@ -104,11 +104,15 @@
     hid = (x * rms_scale(x) * gain[...]).astype(BF)
     hidden[...] = hid
     split_lanes(hid3, hid, hid3.shape[0])
-    for k in range(line):
+
+    def body(k, carry):
         acc = 0.0
         for ref, _, m, at in blocks(near, far):
             acc = acc + mmul(hid3[at], ref[k])
         acc4[s ^ k] = acc
+        return carry
+
+    lax.fori_loop(0, line, body, 0)
     wide = near[0].shape[-1] // 2
     keys = jnp.concatenate([acc4[p, :, :wide] for p in range(line)], 1)
     values = jnp.concatenate([acc4[p, :, wide:] for p in range(line)], 1)
@@ -130,11 +134,15 @@
     s = lax.axis_index("seq")
     cos, sin = tables(cosine, sine)
     split_lanes(hid3, hidden[...], hid3.shape[0])
-    for k in range(line):
+
+    def body(k, carry):
         acc = 0.0
         for ref, _, m, at in blocks(near, far):
             acc = acc + mmul(hid3[at], ref[k, 0])
         acc4[s ^ k] = acc
+        return carry
+
+    lax.fori_loop(0, line, body, 0)
     full = join_lanes(acc4, line)
     for h in range(HEADS):
         u = full[:, head_of(h)]
@@ -175,11 +183,15 @@
         for i in range(GROUPS):
             attn[:, head_of(GROUPS * g + i)] = out[i * piece : (i + 1) * piece]
     split_lanes(att3, attn[...], att3.shape[0])
-    for k in range(line):
+
+    def body(k, carry):
         acc = 0.0
         for ref, _, m, j in blocks(near, far):
             acc = acc + mmul(att3[j], ref[k, 1])
         acc4[s ^ k] = acc
+        return carry
+
+    lax.fori_loop(0, line, body, 0)
     x = rows[...].T + join_lanes(acc4, line)
     mid[...] = x
     hidden[...] = (x * rms_scale(x) * gain[...]).astype(BF)
@@ -199,17 +211,16 @@
 def load_slots(own, right, left, slots):
     s = lax.axis_index("seq")
     line = slots.shape[0]
-    pltpu.sync_copy(own, slots.at[0])
-    for k in range(1, line):
-        for far in range(1, line):
-
-            @pl.when((s ^ k) == s - far)
-            def _():
-                pltpu.sync_copy(right[far - 1], slots.at[k])
-
-            @pl.when((s ^ k) == s + far)
-            def _():
-                pltpu.sync_copy(left[far - 1], slots.at[k])
+    pltpu.sync_copy(own, slots.at[s])
+    for far in range(1, line):
+
+        @pl.when(s >= far)
+        def _():
+            pltpu.sync_copy(right[far - 1], slots.at[s - far])
+
+        @pl.when(s + far < line)
+        def _():
+            pltpu.sync_copy(left[far - 1], slots.at[s + far])
 
 
 def feed_kernel(chips, line, tile, *refs):
@@ -263,10 +274,13 @@
 
 
 def feed_grad_kernel(chips, line, *refs):
-    hid, low, own, right, left, gate_s, up_s, inner_s, down_near, down_far, grads, *scratch = take(
-        refs, 2 * chips, 2 * chips, None, line - 1, line - 1, *[None] * 4, chips, line, *[None] * 5
-    )
-    slots, down_w, hid_s, low_s, sems = scratch
+    hid, low, own, right, left, gate_s, up_s, inner_s, down_near, down_far, *rest = take(
+        refs,
+        *(2 * chips, 2 * chips, None, line - 1, line - 1, None, None, None, None, chips),
+        *(None, line - 1, line - 1, *[None] * 6),
+    )
+    mine, to_left, to_right, slots, down_w, hid_s, low_s, terms, sems = rest
+    s = lax.axis_index("seq")
     copies = load_all(hid, hid_s, sems) + load_all(low, low_s, sems.at[pl.ds(2 * chips, 2 * chips)])
     load_slots(own, right, left, slots)
     piece = hid[0].shape[0]
@@ -284,8 +298,28 @@
     for n, (a, b) in enumerate(((gate_s, hid_s), (up_s, hid_s), (inner_s, low_s))):
         term = left_mmul(a[...], b[...])
         for k in range(line):
-            out = term[k * units : (k + 1) * units]
-            grads[k][n * units : (n + 1) * units] = out.astype(grads[k].dtype)
+            terms[k, n * units : (n + 1) * units] = term[k * units : (k + 1) * units]
+    mine[...] = terms[s]
+    for k in range(1, line):
+        for out, ok, at in (
+            (to_left[k - 1], s >= k, s - k),
+            (to_right[k - 1], s + k < line, s + k),
+        ):
+
+            @pl.when(ok)
+            def _():
+                out[...] = terms[at].astype(BF)
+
+            @pl.when(jnp.logical_not(ok))
+            def _():
+                out[...] = jnp.zeros(out.shape, BF)
+
+
+def add_kernel(*refs):
+    count = len(refs) // 3
+    for i in range(count):
+        a, b, out = refs[2 * i], refs[2 * i + 1], refs[2 * count + i]
+        out[...] = (a[...].astype(F32) + b[...].astype(F32)).astype(BF)
 
 
 def middle_kernel(chips, line, *refs):
@@ -346,11 +380,15 @@
     split_lanes(att3, attn[...], size)
     split_lanes(gq4, grad_query[...], line)
     split_lanes(low4, grad_low[...], line)
-    for ref, core, m, j in blocks(near, far):
-        out = (out_near, out_far)[core][m]
-        for k in range(line):
+
+    def body(k, carry):
+        for ref, core, m, j in blocks(near, far):
+            out = (out_near, out_far)[core][m]
             out[k, 0] = left_mmul(hid3[j], gq4[s ^ k]).astype(BF)
             out[k, 1] = left_mmul(att3[j], low4[s ^ k]).astype(BF)
+        return carry
+
+    lax.fori_loop(0, line, body, 0)
     for ref, _, m, j in blocks(near, far):
         acc = 0.0
         for k in range(line):
@@ -465,9 +503,9 @@
 
 
 def feed_end_kernel(own, *refs):
-    *got, out = refs
-    whole = tree([own[...]] + [g[...].astype(F32) for g in got]).astype(BF)
-    split_lanes(out, whole, out.shape[0])
+    left, right, out = refs
+    whole = own[...] + left[...].astype(F32) + right[...].astype(F32)
+    split_lanes(out, whole.astype(BF), out.shape[0])
 
 
 def feed_done_kernel(got, gate, up, down):
@@ -533,14 +571,14 @@
     return math.prod(outer) * (-(-rows // tile) * tile) * (-(-lanes // 128) * 128) * size
 
 
-def call(kernel, outs, scratch, flops, *args, far=0, far_outs=()):
+def call(kernel, outs, scratch, flops, *args, far=0, far_outs=(), grant=True):
     sizes = [a.size * a.dtype.itemsize for a in (*args, *outs)]
     vmem = pl.BlockSpec(memory_space=pltpu.VMEM)
     free = pl.BlockSpec(memory_space=pl.ANY)
     held = [a for i, a in enumerate(args) if i >= far]
     held += [a for i, a in enumerate(outs) if i not in far_outs]
     held += [array(*x) for x in scratch if isinstance(x, tuple)]
-    limit = min(sum(padded(a) for a in held) + ROOM * 2**20, 60 * 1024 * 2**10)
+    limit = min(sum(padded(a) for a in held) + ROOM * 2**20, 60 * 1024 * 2**10) if grant else None
     return pl.pallas_call(
         kernel,
         out_shape=outs,
@@ -613,6 +651,12 @@
             got.append(held)
         out.append(got)
     return out
+
+
+def hand(x, by, k):
+    n = lax.axis_size("seq")
+    senders = range(n - k) if by > 0 else range(k, n)
+    return lax.ppermute(x, "seq", [(i, i + by) for i in senders])
 
 
 def step(x, by, k):
@@ -662,6 +706,7 @@
         value_weight.T,
         query_weight,
         output_weight,
+        grant=False,
     )
     kv_slots, qo_slots = call(
         functools.partial(stack_kernel, line),
@@ -684,12 +729,13 @@
         gate_weight,
         up_weight,
         down_weight.T,
+        grant=False,
     )
     spread = lax.all_to_all(local, "batch", split_axis=0, concat_axis=0, tiled=True)
     (feed_own,) = call(arrange_kernel, [array((3 * units, width), BF)], [], 1e5, spread)
     feed_right, feed_left = line_chain(feed_own, line)
 
-    (low,) = call(cast_kernel, [array((piece, width), BF)], [], 1e5, grad_rows)
+    (low,) = call(cast_kernel, [array((piece, width), BF)], [], 1e5, grad_rows, grant=False)
     low_near = plane_hops(low, chips)
     low_far = pair_swap(low_near)
 
@@ -770,8 +816,8 @@
         [array(flat, BF)]
         + [array((piece, width), BF)] * chips
         + [array((3 * units, width), F32)]
-        + [array((3 * units, width), BF)] * (line - 1),
-        [*slots, *both, sems],
+        + [array((3 * units, width), BF)] * (2 * line - 2),
+        [*slots, *both, ((line, 3 * units, width), F32), sems],
         8 * tokens * width * line * units,
         *feed_in,
         *acts,
@@ -816,9 +862,24 @@
         down_end_kernel, [array((width, piece), F32)], [], 1e6, mid, down_own, *down_got
     )
 
-    feed_got = [cross(feed_grads[k], k) for k in others]
+    to_left, to_right = feed_grads[1:line], feed_grads[line:]
+    left, right = to_left[-1], to_right[-1]
+    for k in range(line - 1, 0, -1):
+        left = hand(left, -1, k)
+        right = hand(right, 1, k)
+        if k > 1:
+            left, right = call(
+                add_kernel,
+                [array(left.shape, BF)] * 2,
+                [],
+                1e6,
+                left,
+                to_left[k - 2],
+                right,
+                to_right[k - 2],
+            )
     (feed_own,) = call(
-        feed_end_kernel, [array((size, 3 * units, cut), BF)], [], 1e6, feed_grads[0], *feed_got
+        feed_end_kernel, [array((size, 3 * units, cut), BF)], [], 1e6, feed_grads[0], left, right
     )
     feed_back = lax.all_to_all(feed_own, "batch", split_axis=0, concat_axis=0, tiled=True)
     gate_done, up_done, down_done = call(

time: 294 us -> 281 us (0.956)
  waiting for transfers between devices: 133 us -> 105 us
  starting transfers between devices: 80.8 us -> 95.9 us
  Pallas kernels: 48.5 us -> 57.5 us
  local copies, waits for them, and re-layouts: 28 us -> 19.6 us
    ppermute x6, waiting for transfers between devices: 26.8 us -> 8.46 us  [push(): return lax.ppermute(x, 'seq', pairs)]
    ppermute x0 -> x6, starting transfers between devices: none -> 14.8 us  [hand(): return lax.ppermute(x, 'seq', [(i, i + by) for i in senders])]
    ppermute x12 -> x9, waiting for transfers between devices: 33 us -> 20.4 us  [cross(): return lax.ppermute(x, 'seq', [(i, i ^ bits) for i in range(n)])]
    pallas_call x24 -> x26, Pallas kernels: 48.5 us -> 57.5 us  [call(): pl.pallas_call(kernel, out_shape=outs, in_specs=[free if i < far else vme...]
    unnamed x122 -> x98, local copies, waits for them, and re-layouts: 28 us -> 19.6 us
    ppermute x0 -> x6, waiting for transfers between devices: none -> 6.92 us  [hand(): return lax.ppermute(x, 'seq', [(i, i + by) for i in senders])]
    ppermute x56, starting transfers between devices: 32.6 us -> 38 us  [flip(): return lax.ppermute(x, 'batch', [(i, i ^ bits) for i in range(n)])]
    ppermute x12 -> x9, starting transfers between devices: 17.2 us -> 12 us  [cross(): return lax.ppermute(x, 'seq', [(i, i ^ bits) for i in range(n)])]
  transfers between devices with their start and end apart: 82 -> 85, of which waited for: 25 -> 22; matrix products, arithmetic and copies ran while one was open for 0% -> 0% of each run, Pallas kernels for 13% -> 16%
where the time goes in v2:
time: 281 us; the launch traced here: 280 us
  waiting for transfers between devices  105 us (37%)
  starting transfers between devices  95.9 us (34%)
  Pallas kernels  57.5 us (20%)
  local copies, waits for them, and re-layouts  19.6 us (7%)
    pallas_call x26, Pallas kernels, call(): pl.pallas_call(kernel, out_shape=outs, in_specs=[free if i < far else vme...  57.5 us
    ppermute x56, waiting for transfers between devices, flip(): return lax.ppermute(x, 'batch', [(i, i ^ bits) for i in range(n)])  54.2 us
    ppermute x56, starting transfers between devices, flip(): return lax.ppermute(x, 'batch', [(i, i ^ bits) for i in range(n)])  38 us
    ppermute x9, waiting for transfers between devices, cross(): return lax.ppermute(x, 'seq', [(i, i ^ bits) for i in range(n)])  20.4 us
    unnamed x98, local copies, waits for them, and re-layouts  19.6 us
    ppermute x6, waiting for transfers between devices, step(): return lax.ppermute(x, 'seq', [(i, i + by) for i in senders])  15.2 us
    ppermute x6, starting transfers between devices, hand(): return lax.ppermute(x, 'seq', [(i, i + by) for i in senders])  14.8 us
    ppermute x6, starting transfers between devices, push(): return lax.ppermute(x, 'seq', pairs)  13.2 us
  transfers between devices with their start and end apart: 85, of which 22 were waited for; matrix products, arithmetic and copies ran while one was open for 0% of the time, Pallas kernels for 16%

profile of v2, /device:TPU:0, one launch (start us, length us, event | category | flops | bytes accessed | tf_op | source)
XLA Modules:
  0.0 280.0 jit_solution(8293899193407145755)
XLA Ops:
  2.4 5.1 %collective-permute-start.2 = (bf16[120,640]{1,0:T(8,128)(2,1)}, bf16[120,640]{1,0:T(8,128)(2,1)S(1)}, u32[]{:S(2)}, u32[]{:S(2)}) collective-permute-start(bf16[120,640]{1,0:T(8,128)(2,1)} %shard_map.203.refs_0_), channel_id=1, source_target_pairs={{0,3},{1,2},{2,1},{3,0},{4,7},{5,6},{6,5},{7,4},{8,11},{9,10},{10,... | collective-permute-start | bytes 460808 | tf_op jit(solution)/shard_map/ppermute | solution.py:606
  12.6 8.1 %collective-permute-done.1.refs_2_ = bf16[120,640]{1,0:T(8,128)(2,1)S(1)} collective-permute-done((bf16[120,640]{1,0:T(8,128)(2,1)}, bf16[120,640]{1,0:T(8,128)(2,1)S(1)}, u32[]{:S(2)}, u32[]{:S(2)}) %collective-permute-start.1) | collective-permute-done | bytes 153632 | tf_op jit(solution)/shard_map/ppermute | solution.py:606
  25.5 6.3 %collective-permute-done.5.refs_8_.refs_15_ = bf16[4,120,160]{2,1,0:T(8,128)(2,1)S(1)} collective-permute-done((bf16[4,120,160]{2,1,0:T(8,128)(2,1)S(1)}, bf16[4,120,160]{2,1,0:T(8,128)(2,1)S(1)}, u32[]{:S(2)}, u32[]{:S(2)}) %collective-permute-start.5) | collective-permute-done | bytes 153632 | tf_op jit(solution)/shard_map/ppermute | solution.py:601
  38.5 4.1 %all-to-all-start = ((bf16[8,3,80,120]{3,2,1,0:T(8,128)(2,1)}), bf16[8,3,80,120]{3,2,1,0:T(8,128)(2,1)}, u32[]{:S(2)}, u32[]{:S(2)}) async-start(bf16[8,3,80,120]{3,2,1,0:T(8,128)(2,1)} %shard_map.209), calls=%async_computation | async-start | bytes 983040 | tf_op jit(solution)/shard_map/all_to_all | solution.py:734
  61.2 7.5 %collective-permute-done.29.refs_11_ = bf16[128,960]{1,0:T(8,128)(2,1)S(1)} collective-permute-done((bf16[128,960]{1,0:T(8,128)(2,1)}, bf16[128,960]{1,0:T(8,128)(2,1)S(1)}, u32[]{:S(2)}, u32[]{:S(2)}) %collective-permute-start.29) | collective-permute-done | bytes 245792 | tf_op jit(solution)/shard_map/ppermute | solution.py:601
  68.7 4.9 %collective-permute-start.19 = (bf16[136,640]{1,0:T(8,128)(2,1)S(1)}, bf16[136,640]{1,0:T(8,128)(2,1)}, u32[]{:S(2)}, u32[]{:S(2)}) collective-permute-start(bf16[136,640]{1,0:T(8,128)(2,1)S(1)} %get-tuple-element.106.refs_1_.refs_20_), channel_id=1, source_target_pairs={{0,3},{4,7},{8,11},{12,15},{16,19},{20,23},{24,27},{28,31}} | collective-permute-start | bytes 522248 | tf_op jit(solution)/shard_map/ppermute | solution.py:612
  80.6 4.6 %collective-permute-start.34 = (bf16[240,960]{1,0:T(8,128)(2,1)S(1)}, bf16[240,960]{1,0:T(8,128)(2,1)S(1)}, u32[]{:S(2)}, u32[]{:S(2)}) collective-permute-start(bf16[240,960]{1,0:T(8,128)(2,1)S(1)} %shard_map.210.refs_16_), channel_id=1, source_target_pairs={{0,1},{1,2},{2,3},{4,5},{5,6},{6,7},{8,9},{9,10},{10,11},{12,13},{... | collective-permute-start | bytes 1382408 | tf_op jit(solution)/shard_map/ppermute | solution.py:665
  85.9 6.9 %collective-permute-done.37.refs_20_ = bf16[240,960]{1,0:T(8,128)(2,1)S(1)} collective-permute-done((bf16[240,960]{1,0:T(8,128)(2,1)S(1)}, bf16[240,960]{1,0:T(8,128)(2,1)S(1)}, u32[]{:S(2)}, u32[]{:S(2)}) %collective-permute-start.37) | collective-permute-done | bytes 460832 | tf_op jit(solution)/shard_map/ppermute | solution.py:665
  99.9 6.0 %shard_map.207 = (f32[5,384,512]{2,1,0:T(8,128)S(1)}, bf16[128,960]{1,0:T(8,128)(2,1)S(1)}, f32[128,960]{1,0:T(8,128)S(1)}, bf16[128,960]{1,0:T(8,128)(2,1)S(1)}) custom-call(bf16[128,960]{1,0:T(8,128)(2,1)S(1)} %shard_map.206.refs_0_.refs_8_, bf16[136,640]{1,0:T(8,128)(2,1)S(1)} %get-tuple-element.106.refs_1_.refs_20_, ...), custom_call_target="tpu_custom_call" | custom-call | flops 487587840 | bytes 10039552 | tf_op jit(solution)/shard_map/pallas_call | solution.py:582
  117.7 5.0 %collective-permute-done.21.refs_2_ = bf16[128,960]{1,0:T(8,128)(2,1)S(1)} collective-permute-done((bf16[128,960]{1,0:T(8,128)(2,1)S(1)}, bf16[128,960]{1,0:T(8,128)(2,1)S(1)}, u32[]{:S(2)}, u32[]{:S(2)}) %collective-permute-start.21) | collective-permute-done | bytes 245792 | tf_op jit(solution)/shard_map/ppermute | solution.py:601
  124.6 6.2 %collective-permute-done.39.refs_22_ = bf16[240,960]{1,0:T(8,128)(2,1)S(1)} collective-permute-done((bf16[240,960]{1,0:T(8,128)(2,1)S(1)}, bf16[240,960]{1,0:T(8,128)(2,1)S(1)}, u32[]{:S(2)}, u32[]{:S(2)}) %collective-permute-start.39) | collective-permute-done | bytes 460832 | tf_op jit(solution)/shard_map/ppermute | solution.py:665
  130.8 9.0 %shard_map.211 = (bf16[512,960]{1,0:T(8,128)(2,1)S(1)}, bf16[128,960]{1,0:T(8,128)(2,1)S(1)}, bf16[128,960]{1,0:T(8,128)(2,1)S(1)}, bf16[128,960]{1,0:T(8,128)(2...) custom-call(bf16[128,960]{1,0:T(8,128)(2,1)S(1)} %get-tuple-element., ...), custom_call_target="tpu_custom_call" | custom-call | flops 3145728000 | bytes 11089920 | tf_op jit(solution)/shard_map/pallas_call | solution.py:582
  140.8 5.8 %shard_map.212 = (bf16[512,960]{1,0:T(8,128)(2,1)S(1)}, bf16[128,960]{1,0:T(8,128)(2,1)S(1)}, bf16[128,960]{1,0:T(8,128)(2,1)S(1)}, bf16[128,960]{1,0:T(8,128)(2...) custom-call(bf16[128,960]{1,0:T(8,128)(2,1)S(1)} %get-tuple-element., ...), custom_call_target="tpu_custom_call" | custom-call | flops 2516582400 | bytes 14776320 | tf_op jit(solution)/shard_map/pallas_call | solution.py:582
  154.6 6.9 %collective-permute-done.78.refs_2_ = bf16[240,960]{1,0:T(8,128)(2,1)S(1)} collective-permute-done((bf16[240,960]{1,0:T(8,128)(2,1)S(1)}, bf16[240,960]{1,0:T(8,128)(2,1)S(1)}, u32[]{:S(2)}, u32[]{:S(2)}) %collective-permute-start.78) | collective-permute-done | bytes 460832 | tf_op jit(solution)/shard_map/ppermute | solution.py:659
  166.1 6.2 %shard_map.216 = (f32[128,960]{1,0:T(8,128)S(1)}, f32[1,960]{1,0:T(1,128)S(1)}, bf16[128,960]{1,0:T(8,128)(2,1)S(1)}, bf16[128,960]{1,0:T(8,128)(2,1)S(1)}, f32[...) custom-call(f32[128,960]{1,0:T(8,128)S(1)} %get-tuple-element.126.re, ...), custom_call_target="tpu_custom_call" | custom-call | flops 739246080 | bytes 12860928 | tf_op jit(solution)/shard_map/pallas_call | solution.py:582
  176.3 4.0 %collective-permute-start.80 = (bf16[240,960]{1,0:T(8,128)(2,1)S(1)}, bf16[240,960]{1,0:T(8,128)(2,1)S(1)}, u32[]{:S(2)}, u32[]{:S(2)}) collective-permute-start(bf16[240,960]{1,0:T(8,128)(2,1)S(1)} %get-tuple-element.188), channel_id=1, source_target_pairs={{0,1},{1,2},{4,5},{5,6},{8,9},{9,10},{12,13},{13,14},{16,17},{17,1... | collective-permute-start | bytes 1382408 | tf_op jit(solution)/shard_map/ppermute | solution.py:659
  183.6 8.4 %collective-permute-done.55.refs_2_ = bf16[128,640]{1,0:T(8,128)(2,1)S(1)} collective-permute-done((bf16[128,640]{1,0:T(8,128)(2,1)S(1)}, bf16[128,640]{1,0:T(8,128)(2,1)S(1)}, u32[]{:S(2)}, u32[]{:S(2)}) %collective-permute-start.55) | collective-permute-done | bytes 163872 | tf_op jit(solution)/shard_map/ppermute | solution.py:612
  196.2 4.6 %collective-permute-start.82 = (bf16[240,960]{1,0:T(8,128)(2,1)S(1)}, bf16[240,960]{1,0:T(8,128)(2,1)S(1)}, u32[]{:S(2)}, u32[]{:S(2)}) collective-permute-start(bf16[240,960]{1,0:T(8,128)(2,1)S(1)} %get-tuple-element.191), channel_id=1, source_target_pairs={{0,1},{1,2},{2,3},{4,5},{5,6},{6,7},{8,9},{9,10},{10,11},{12,13},{... | collective-permute-start | bytes 1382408 | tf_op jit(solution)/shard_map/ppermute | solution.py:659
  213.7 3.9 %all-to-all-start.1 = ((bf16[8,240,120]{2,1,0:T(8,128)(2,1)}), bf16[8,240,120]{2,1,0:T(8,128)(2,1)S(1)}, u32[]{:S(2)}, u32[]{:S(2)}) async-start(bf16[8,240,120]{2,1,0:T(8,128)(2,1)} %shard_map.227), calls=%async_computation.1 | async-start | bytes 983040 | tf_op jit(solution)/shard_map/all_to_all | solution.py:884
  229.6 5.8 %collective-permute-done.72.refs_1_ = bf16[4,2,120,240]{3,2,1,0:T(8,128)(2,1)} collective-permute-done((bf16[4,2,120,240]{3,2,1,0:T(8,128)(2,1)}, bf16[4,2,120,240]{3,2,1,0:T(8,128)(2,1)}, u32[]{:S(2)}, u32[]{:S(2)}) %collective-permute-start.72) | collective-permute-done | bytes 460832 | tf_op jit(solution)/shard_map/ppermute | solution.py:601
  235.5 4.1 %collective-permute-start.63 = (bf16[496,160]{1,0:T(8,128)(2,1)S(1)}, bf16[496,160]{1,0:T(8,128)(2,1)S(1)}, u32[]{:S(2)}, u32[]{:S(2)}) collective-permute-start(bf16[496,160]{1,0:T(8,128)(2,1)S(1)} %get-tuple-element.153), channel_id=1, source_target_pairs={{0,24},{4,28},{8,16},{12,20},{16,8},{20,12},{24,0},{28,4},{1,25},{... | collective-permute-start | bytes 476168 | tf_op jit(solution)/shard_map/ppermute | solution.py:601
  241.1 7.2 %collective-permute-done.61.refs_0_ = bf16[496,160]{1,0:T(8,128)(2,1)S(1)} collective-permute-done((bf16[496,160]{1,0:T(8,128)(2,1)S(1)}, bf16[496,160]{1,0:T(8,128)(2,1)S(1)}, u32[]{:S(2)}, u32[]{:S(2)}) %collective-permute-start.61) | collective-permute-done | bytes 158752 | tf_op jit(solution)/shard_map/ppermute | solution.py:601
  248.3 11.5 %collective-permute-done.62.refs_1_ = bf16[496,160]{1,0:T(8,128)(2,1)S(1)} collective-permute-done((bf16[496,160]{1,0:T(8,128)(2,1)S(1)}, bf16[496,160]{1,0:T(8,128)(2,1)S(1)}, u32[]{:S(2)}, u32[]{:S(2)}) %collective-permute-start.62) | collective-permute-done | bytes 158752 | tf_op jit(solution)/shard_map/ppermute | solution.py:601
  270.6 6.4 %collective-permute-done.65.refs_1_ = bf16[136,160]{1,0:T(8,128)(2,1)S(1)} collective-permute-done((bf16[136,160]{1,0:T(8,128)(2,1)S(1)}, bf16[136,160]{1,0:T(8,128)(2,1)S(1)}, u32[]{:S(2)}, u32[]{:S(2)}) %collective-permute-start.65) | collective-permute-done | bytes 43552 | tf_op jit(solution)/shard_map/ppermute | solution.py:606
  (273 shorter events, 130.3 us)
Async XLA Ops:
  10.0 32.7 %collective-permute-start.30 = (bf16[128,960]{1,0:T(8,128)(2,1)}, bf16[128,960]{1,0:T(8,128)(2,1)}, u32[]{:S(2)}, u32[]{:S(2)}) collective-permute-start(bf16[128,960]{1,0:T(8,128)(2,1)} %shard_map.208.refs_8_), channel_id=1, source_target_pairs={{0,4},{4,0},{8,12},{12,8},{16,20},{20,16},{24,28},{28,24},{1,5},{5... | collective-permute-start | bytes 737288 | tf_op jit(solution)/shard_map/ppermute | solution.py:601
  25.5 17.6 %collective-permute-start.6 = (bf16[4,120,160]{2,1,0:T(8,128)(2,1)S(1)}, bf16[4,120,160]{2,1,0:T(8,128)(2,1)S(1)}, u32[]{:S(2)}, u32[]{:S(2)}) collective-permute-start(bf16[4,120,160]{2,1,0:T(8,128)(2,1)S(1)} %get-tuple-element.103.refs_5_.refs_12_), channel_id=1, source_target_pairs={{0,4},{4,0},{8,12},{12,8},{16,20},{20,16},{24,28},{28,24},{1,5},{5... | collective-permute-start | bytes 460808 | tf_op jit(solution)/shard_map/ppermute | solution.py:601
  38.5 39.5 %all-to-all-start = ((bf16[8,3,80,120]{3,2,1,0:T(8,128)(2,1)}), bf16[8,3,80,120]{3,2,1,0:T(8,128)(2,1)}, u32[]{:S(2)}, u32[]{:S(2)}) async-start(bf16[8,3,80,120]{3,2,1,0:T(8,128)(2,1)} %shard_map.209), calls=%async_computation | async-start | bytes 983040 | tf_op jit(solution)/shard_map/all_to_all | solution.py:734
  42.7 30.8 %collective-permute-start.13 = (bf16[4,2,120,240]{3,2,1,0:T(8,128)(2,1)S(1)}, bf16[4,2,120,240]{3,2,1,0:T(8,128)(2,1)S(1)}, u32[]{:S(2)}, u32[]{:S(2)}) collective-permute-start(bf16[4,2,120,240]{3,2,1,0:T(8,128)(2,1)S(1)} %get-tuple-element.105.refs_3_.refs_8_.refs_12_.refs_4_), channel_id=1, source_target_pairs={{0,4},{4,0},{8,12},{12,8},{16,20},{20,16},{24,28},{28,24},{1,5},{5... | collective-permute-start | bytes 1382408 | tf_op jit(solution)/shard_map/ppermute | solution.py:601
  43.8 31.7 %collective-permute-start.12 = (bf16[4,2,120,240]{3,2,1,0:T(8,128)(2,1)S(1)}, bf16[4,2,120,240]{3,2,1,0:T(8,128)(2,1)S(1)}, u32[]{:S(2)}, u32[]{:S(2)}) collective-permute-start(bf16[4,2,120,240]{3,2,1,0:T(8,128)(2,1)S(1)} %get-tuple-element.105.refs_3_.refs_8_.refs_12_.refs_4_), channel_id=1, source_target_pairs={{0,24},{4,28},{8,16},{12,20},{16,8},{20,12},{24,0},{28,4},{1,25},{... | collective-permute-start | bytes 1382408 | tf_op jit(solution)/shard_map/ppermute | solution.py:601
  47.1 21.6 %collective-permute-start.29 = (bf16[128,960]{1,0:T(8,128)(2,1)}, bf16[128,960]{1,0:T(8,128)(2,1)S(1)}, u32[]{:S(2)}, u32[]{:S(2)}) collective-permute-start(bf16[128,960]{1,0:T(8,128)(2,1)} %shard_map.208.refs_8_), channel_id=1, source_target_pairs={{0,24},{4,28},{8,16},{12,20},{16,8},{20,12},{24,0},{28,4},{1,25},{... | collective-permute-start | bytes 737288 | tf_op jit(solution)/shard_map/ppermute | solution.py:601
  47.5 31.9 %collective-permute-start.11 = (bf16[4,2,120,240]{3,2,1,0:T(8,128)(2,1)S(1)}, bf16[4,2,120,240]{3,2,1,0:T(8,128)(2,1)S(1)}, u32[]{:S(2)}, u32[]{:S(2)}) collective-permute-start(bf16[4,2,120,240]{3,2,1,0:T(8,128)(2,1)S(1)} %get-tuple-element.105.refs_3_.refs_8_.refs_12_.refs_4_), channel_id=1, source_target_pairs={{0,16},{4,20},{8,24},{12,28},{16,0},{20,4},{24,8},{28,12},{1,17},{... | collective-permute-start | bytes 1382408 | tf_op jit(solution)/shard_map/ppermute | solution.py:601
  49.2 31.4 %collective-permute-start.10 = (bf16[4,2,120,240]{3,2,1,0:T(8,128)(2,1)S(1)}, bf16[4,2,120,240]{3,2,1,0:T(8,128)(2,1)S(1)}, u32[]{:S(2)}, u32[]{:S(2)}) collective-permute-start(bf16[4,2,120,240]{3,2,1,0:T(8,128)(2,1)S(1)} %get-tuple-element.105.refs_3_.refs_8_.refs_12_.refs_4_), channel_id=1, source_target_pairs={{0,8},{4,12},{8,0},{12,4},{16,24},{20,28},{24,16},{28,20},{1,9},{5... | collective-permute-start | bytes 1382408 | tf_op jit(solution)/shard_map/ppermute | solution.py:601
  95.5 17.7 %collective-permute-start.38 = (bf16[240,960]{1,0:T(8,128)(2,1)S(1)}, bf16[240,960]{1,0:T(8,128)(2,1)S(1)}, u32[]{:S(2)}, u32[]{:S(2)}) collective-permute-start(bf16[240,960]{1,0:T(8,128)(2,1)S(1)} %collective-permute-done.37.refs_20_), channel_id=1, source_target_pairs={{1,0},{2,1},{5,4},{6,5},{9,8},{10,9},{13,12},{14,13},{17,16},{18,1... | collective-permute-start | bytes 1382408 | tf_op jit(solution)/shard_map/ppermute | solution.py:665
  96.8 17.7 %collective-permute-start.35 = (bf16[240,960]{1,0:T(8,128)(2,1)S(1)}, bf16[240,960]{1,0:T(8,128)(2,1)S(1)}, u32[]{:S(2)}, u32[]{:S(2)}) collective-permute-start(bf16[240,960]{1,0:T(8,128)(2,1)S(1)} %collective-permute-done.34.refs_17_), channel_id=1, source_target_pairs={{1,2},{2,3},{5,6},{6,7},{9,10},{10,11},{13,14},{14,15},{17,18},{18... | collective-permute-start | bytes 1382408 | tf_op jit(solution)/shard_map/ppermute | solution.py:665
  154.6 17.7 %collective-permute-start.40 = (bf16[128,960]{1,0:T(8,128)(2,1)S(1)}, bf16[128,960]{1,0:T(8,128)(2,1)S(1)}, u32[]{:S(2)}, u32[]{:S(2)}) collective-permute-start(bf16[128,960]{1,0:T(8,128)(2,1)S(1)} %get-tuple-element.113), channel_id=1, source_target_pairs={{0,4},{4,0},{8,12},{12,8},{16,20},{20,16},{24,28},{28,24},{1,5},{5... | collective-permute-start | bytes 737288 | tf_op jit(solution)/shard_map/ppermute | solution.py:601
  161.8 30.8 %collective-permute-start.79 = (bf16[240,960]{1,0:T(8,128)(2,1)S(1)}, bf16[240,960]{1,0:T(8,128)(2,1)S(1)}, u32[]{:S(2)}, u32[]{:S(2)}) collective-permute-start(bf16[240,960]{1,0:T(8,128)(2,1)S(1)} %get-tuple-element.186), channel_id=1, source_target_pairs={{2,1},{3,2},{6,5},{7,6},{10,9},{11,10},{14,13},{15,14},{18,17},{19... | collective-permute-start | bytes 1382408 | tf_op jit(solution)/shard_map/ppermute | solution.py:659
  173.6 18.4 %collective-permute-start.55 = (bf16[128,640]{1,0:T(8,128)(2,1)S(1)}, bf16[128,640]{1,0:T(8,128)(2,1)S(1)}, u32[]{:S(2)}, u32[]{:S(2)}) collective-permute-start(bf16[128,640]{1,0:T(8,128)(2,1)S(1)} %get-tuple-element.134), channel_id=1, source_target_pairs={{2,0},{3,1},{6,4},{7,5},{10,8},{11,9},{14,12},{15,13},{18,16},{19,... | collective-permute-start | bytes 491528 | tf_op jit(solution)/shard_map/ppermute | solution.py:612
  207.1 22.1 %collective-permute-start.71 = (bf16[4,2,120,240]{3,2,1,0:T(8,128)(2,1)}, bf16[4,2,120,240]{3,2,1,0:T(8,128)(2,1)}, u32[]{:S(2)}, u32[]{:S(2)}) collective-permute-start(bf16[4,2,120,240]{3,2,1,0:T(8,128)(2,1)} %get-tuple-element.169), channel_id=1, source_target_pairs={{0,8},{4,12},{8,0},{12,4},{16,24},{20,28},{24,16},{28,20},{1,9},{5... | collective-permute-start | bytes 1382408 | tf_op jit(solution)/shard_map/ppermute | solution.py:601
  208.8 26.7 %collective-permute-start.72 = (bf16[4,2,120,240]{3,2,1,0:T(8,128)(2,1)}, bf16[4,2,120,240]{3,2,1,0:T(8,128)(2,1)}, u32[]{:S(2)}, u32[]{:S(2)}) collective-permute-start(bf16[4,2,120,240]{3,2,1,0:T(8,128)(2,1)} %get-tuple-element.170), channel_id=1, source_target_pairs={{0,16},{4,20},{8,24},{12,28},{16,0},{20,4},{24,8},{28,12},{1,17},{... | collective-permute-start | bytes 1382408 | tf_op jit(solution)/shard_map/ppermute | solution.py:601
  210.3 25.2 %collective-permute-start.73 = (bf16[4,2,120,240]{3,2,1,0:T(8,128)(2,1)}, bf16[4,2,120,240]{3,2,1,0:T(8,128)(2,1)}, u32[]{:S(2)}, u32[]{:S(2)}) collective-permute-start(bf16[4,2,120,240]{3,2,1,0:T(8,128)(2,1)} %get-tuple-element.171), channel_id=1, source_target_pairs={{0,24},{4,28},{8,16},{12,20},{16,8},{20,12},{24,0},{28,4},{1,25},{... | collective-permute-start | bytes 1382408 | tf_op jit(solution)/shard_map/ppermute | solution.py:601
  213.7 65.0 %all-to-all-start.1 = ((bf16[8,240,120]{2,1,0:T(8,128)(2,1)}), bf16[8,240,120]{2,1,0:T(8,128)(2,1)S(1)}, u32[]{:S(2)}, u32[]{:S(2)}) async-start(bf16[8,240,120]{2,1,0:T(8,128)(2,1)} %shard_map.227), calls=%async_computation.1 | async-start | bytes 983040 | tf_op jit(solution)/shard_map/all_to_all | solution.py:884
  218.3 44.0 %collective-permute-start.45 = (bf16[128,960]{1,0:T(8,128)(2,1)}, bf16[128,960]{1,0:T(8,128)(2,1)S(1)}, u32[]{:S(2)}, u32[]{:S(2)}) collective-permute-start(bf16[128,960]{1,0:T(8,128)(2,1)} %copy-done.48), channel_id=1, source_target_pairs={{0,16},{4,20},{8,24},{12,28},{16,0},{20,4},{24,8},{28,12},{1,17},{... | collective-permute-start | bytes 737288 | tf_op jit(solution)/shard_map/ppermute | solution.py:601
  219.9 43.6 %collective-permute-start.46 = (bf16[128,960]{1,0:T(8,128)(2,1)}, bf16[128,960]{1,0:T(8,128)(2,1)S(1)}, u32[]{:S(2)}, u32[]{:S(2)}) collective-permute-start(bf16[128,960]{1,0:T(8,128)(2,1)} %copy-done.47), channel_id=1, source_target_pairs={{0,24},{4,28},{8,16},{12,20},{16,8},{20,12},{24,0},{28,4},{1,25},{... | collective-permute-start | bytes 737288 | tf_op jit(solution)/shard_map/ppermute | solution.py:601
  229.2 19.1 %collective-permute-start.61 = (bf16[496,160]{1,0:T(8,128)(2,1)S(1)}, bf16[496,160]{1,0:T(8,128)(2,1)S(1)}, u32[]{:S(2)}, u32[]{:S(2)}) collective-permute-start(bf16[496,160]{1,0:T(8,128)(2,1)S(1)} %get-tuple-element.151), channel_id=1, source_target_pairs={{0,8},{4,12},{8,0},{12,4},{16,24},{20,28},{24,16},{28,20},{1,9},{5... | collective-permute-start | bytes 476168 | tf_op jit(solution)/shard_map/ppermute | solution.py:601
  235.4 24.4 %collective-permute-start.62 = (bf16[496,160]{1,0:T(8,128)(2,1)S(1)}, bf16[496,160]{1,0:T(8,128)(2,1)S(1)}, u32[]{:S(2)}, u32[]{:S(2)}) collective-permute-start(bf16[496,160]{1,0:T(8,128)(2,1)S(1)} %get-tuple-element.152), channel_id=1, source_target_pairs={{0,16},{4,20},{8,24},{12,28},{16,0},{20,4},{24,8},{28,12},{1,17},{... | collective-permute-start | bytes 476168 | tf_op jit(solution)/shard_map/ppermute | solution.py:601
  235.5 24.9 %collective-permute-start.63 = (bf16[496,160]{1,0:T(8,128)(2,1)S(1)}, bf16[496,160]{1,0:T(8,128)(2,1)S(1)}, u32[]{:S(2)}, u32[]{:S(2)}) collective-permute-start(bf16[496,160]{1,0:T(8,128)(2,1)S(1)} %get-tuple-element.153), channel_id=1, source_target_pairs={{0,24},{4,28},{8,16},{12,20},{16,8},{20,12},{24,0},{28,4},{1,25},{... | collective-permute-start | bytes 476168 | tf_op jit(solution)/shard_map/ppermute | solution.py:601
  248.3 29.5 %collective-permute-start.74 = (bf16[2,120,240]{2,1,0:T(8,128)(2,1)S(1)}, bf16[2,120,240]{2,1,0:T(8,128)(2,1)S(1)}, u32[]{:S(2)}, u32[]{:S(2)}) collective-permute-start(bf16[2,120,240]{2,1,0:T(8,128)(2,1)S(1)} %get-tuple-element.173), channel_id=1, source_target_pairs={{0,1},{1,0},{2,3},{3,2},{4,5},{5,4},{6,7},{7,6},{8,9},{9,8},{10,11... | collective-permute-start | bytes 345608 | tf_op jit(solution)/shard_map/ppermute | solution.py:606
  259.8 18.1 %collective-permute-start.75 = (bf16[2,120,240]{2,1,0:T(8,128)(2,1)S(1)}, bf16[2,120,240]{2,1,0:T(8,128)(2,1)S(1)}, u32[]{:S(2)}, u32[]{:S(2)}) collective-permute-start(bf16[2,120,240]{2,1,0:T(8,128)(2,1)S(1)} %get-tuple-element.174), channel_id=1, source_target_pairs={{0,2},{1,3},{2,0},{3,1},{4,6},{5,7},{6,4},{7,5},{8,10},{9,11},{10,... | collective-permute-start | bytes 345608 | tf_op jit(solution)/shard_map/ppermute | solution.py:606
  (110 other events, 1326.9 us)

commit v3 on v2

--- a/solution.py
+++ b/solution.py
@@ -197,15 +197,10 @@
     hidden[...] = (x * rms_scale(x) * gain[...]).astype(BF)
 
 
-def load_all(refs, scratch, sems):
+def load_all(refs, scratch):
     rows = refs[0].shape[0]
-    copies = [
-        pltpu.make_async_copy(ref, scratch.at[pl.ds(i * rows, rows)], sems.at[i])
-        for i, ref in enumerate(refs)
-    ]
-    for copy in copies:
-        copy.start()
-    return copies
+    for i, ref in enumerate(refs):
+        scratch[i * rows : (i + 1) * rows] = ref[...]
 
 
 def load_slots(own, right, left, slots):
@@ -225,11 +220,12 @@
 
 def feed_kernel(chips, line, tile, *refs):
     hid, low, own, right, left, back_near, back_far, gate_s, up_s, inner_s, *scratch = take(
-        refs, 2 * chips, 2 * chips, None, line - 1, line - 1, None, chips, *[None] * 12
-    )
-    slots, gate_w, up_w, down_w, hid_s, low_s, far_s, sems, far_sems = scratch
-    copies = load_all(hid, hid_s, sems) + load_all(low, low_s, sems.at[pl.ds(2 * chips, 2 * chips)])
+        refs, 2 * chips, 2 * chips, None, line - 1, line - 1, None, chips, *[None] * 11
+    )
+    slots, gate_w, up_w, down_w, hid_s, low_s, far_s, far_sems = scratch
     load_slots(own, right, left, slots)
+    load_all(hid, hid_s)
+    load_all(low, low_s)
     piece = hid[0].shape[0]
     units = own.shape[0] // 3
     for k in range(line):
@@ -237,8 +233,6 @@
         gate_w[span] = slots[k, :units]
         up_w[span] = slots[k, units : 2 * units]
         down_w[span] = slots[k, 2 * units :]
-    for copy in copies:
-        copy.wait()
     half = chips * piece
 
     def run(back, base):
@@ -277,18 +271,17 @@
     hid, low, own, right, left, gate_s, up_s, inner_s, down_near, down_far, *rest = take(
         refs,
         *(2 * chips, 2 * chips, None, line - 1, line - 1, None, None, None, None, chips),
-        *(None, line - 1, line - 1, *[None] * 6),
-    )
-    mine, to_left, to_right, slots, down_w, hid_s, low_s, terms, sems = rest
+        *(None, line - 1, line - 1, *[None] * 5),
+    )
+    mine, to_left, to_right, slots, down_w, hid_s, low_s, terms = rest
     s = lax.axis_index("seq")
-    copies = load_all(hid, hid_s, sems) + load_all(low, low_s, sems.at[pl.ds(2 * chips, 2 * chips)])
     load_slots(own, right, left, slots)
+    load_all(hid, hid_s)
+    load_all(low, low_s)
     piece = hid[0].shape[0]
     units = own.shape[0] // 3
     for k in range(line):
         down_w[k * units : (k + 1) * units] = slots[k, 2 * units :]
-    for copy in copies:
-        copy.wait()
     half = chips * piece
     for m in range(chips):
         span = slice(m * piece, (m + 1) * piece)
@@ -571,18 +564,18 @@
     return math.prod(outer) * (-(-rows // tile) * tile) * (-(-lanes // 128) * 128) * size
 
 
-def call(kernel, outs, scratch, flops, *args, far=0, far_outs=(), grant=True):
+def call(kernel, outs, scratch, flops, *args, far=(), far_outs=(), grant=True):
     sizes = [a.size * a.dtype.itemsize for a in (*args, *outs)]
     vmem = pl.BlockSpec(memory_space=pltpu.VMEM)
     free = pl.BlockSpec(memory_space=pl.ANY)
-    held = [a for i, a in enumerate(args) if i >= far]
+    held = [a for i, a in enumerate(args) if i not in far]
     held += [a for i, a in enumerate(outs) if i not in far_outs]
     held += [array(*x) for x in scratch if isinstance(x, tuple)]
     limit = min(sum(padded(a) for a in held) + ROOM * 2**20, 60 * 1024 * 2**10) if grant else None
     return pl.pallas_call(
         kernel,
         out_shape=outs,
-        in_specs=[free if i < far else vmem for i in range(len(args))],
+        in_specs=[free if i in far else vmem for i in range(len(args))],
         out_specs=[free if i in far_outs else vmem for i in range(len(outs))],
         scratch_shapes=[x if not isinstance(x, tuple) else pltpu.VMEM(x[0], x[1]) for x in scratch],
         cost_estimate=pl.CostEstimate(
@@ -790,7 +783,7 @@
     feed_in = [*hid_near, *hid_far, *low_near, *low_far, feed_own, *feed_right, *feed_left]
     slots = [((line, 3 * units, width), BF), ((line * units, width), BF)]
     both = [((tokens, width), BF)] * 2
-    sems = pltpu.SemaphoreType.DMA((4 * chips,))
+    kept = range(4 * chips, len(feed_in))
     back_near, *rest = call(
         functools.partial(feed_kernel, chips, line, 2 * piece),
         [array(flat, BF)] + [array((piece, width), BF)] * chips + [array(act, BF)] * 3,
@@ -801,12 +794,11 @@
             slots[1],
             *both,
             (flat, BF),
-            sems,
             pltpu.SemaphoreType.DMA((chips,)),
         ],
         10 * tokens * width * line * units,
         *feed_in,
-        far=len(feed_in),
+        far=kept,
         far_outs=range(1, chips + 1),
     )
     back_far, acts = rest[:chips], rest[chips:]
@@ -817,11 +809,11 @@
         + [array((piece, width), BF)] * chips
         + [array((3 * units, width), F32)]
         + [array((3 * units, width), BF)] * (2 * line - 2),
-        [*slots, *both, ((line, 3 * units, width), F32), sems],
+        [*slots, *both, ((line, 3 * units, width), F32)],
         8 * tokens * width * line * units,
         *feed_in,
         *acts,
-        far=len(feed_in),
+        far=kept,
     )
     down_far, feed_grads = rest[:chips], rest[chips:]
     grad_mid, feed_term, grad_mid_low, grad_query, kv_own, *kv_sent = call(

time: 281 us -> 282 us (level)
  no operation moved by 1% of the time
where the time goes in v3:
time: 282 us; the launch traced here: 281 us
  waiting for transfers between devices  105 us (37%)
  starting transfers between devices  95.8 us (34%)
  Pallas kernels  58.2 us (21%)
  local copies, waits for them, and re-layouts  19.6 us (7%)
    pallas_call x26, Pallas kernels, call(): pl.pallas_call(kernel, out_shape=outs, in_specs=[free if i in far else vm...  58.2 us
    ppermute x56, waiting for transfers between devices, flip(): return lax.ppermute(x, 'batch', [(i, i ^ bits) for i in range(n)])  54.2 us
    ppermute x56, starting transfers between devices, flip(): return lax.ppermute(x, 'batch', [(i, i ^ bits) for i in range(n)])  38 us
    ppermute x9, waiting for transfers between devices, cross(): return lax.ppermute(x, 'seq', [(i, i ^ bits) for i in range(n)])  20.6 us
    unnamed x98, local copies, waits for them, and re-layouts  19.6 us
    ppermute x6, waiting for transfers between devices, step(): return lax.ppermute(x, 'seq', [(i, i + by) for i in senders])  15.2 us
    ppermute x6, starting transfers between devices, hand(): return lax.ppermute(x, 'seq', [(i, i + by) for i in senders])  14.8 us
    ppermute x6, starting transfers between devices, push(): return lax.ppermute(x, 'seq', pairs)  13.2 us
  transfers between devices with their start and end apart: 85, of which 22 were waited for; matrix products, arithmetic and copies ran while one was open for 0% of the time, Pallas kernels for 16%

profile of v3, /device:TPU:0, one launch (start us, length us, event | category | flops | bytes accessed | tf_op | source)
XLA Modules:
  0.0 280.7 jit_solution(2098372593270616134)
XLA Ops:
  2.4 5.1 %collective-permute-start.2 = (bf16[120,640]{1,0:T(8,128)(2,1)}, bf16[120,640]{1,0:T(8,128)(2,1)S(1)}, u32[]{:S(2)}, u32[]{:S(2)}) collective-permute-start(bf16[120,640]{1,0:T(8,128)(2,1)} %shard_map.203.refs_0_), channel_id=1, source_target_pairs={{0,3},{1,2},{2,1},{3,0},{4,7},{5,6},{6,5},{7,4},{8,11},{9,10},{10,... | collective-permute-start | bytes 460808 | tf_op jit(solution)/shard_map/ppermute | solution.py:599
  12.6 8.1 %collective-permute-done.1.refs_2_ = bf16[120,640]{1,0:T(8,128)(2,1)S(1)} collective-permute-done((bf16[120,640]{1,0:T(8,128)(2,1)}, bf16[120,640]{1,0:T(8,128)(2,1)S(1)}, u32[]{:S(2)}, u32[]{:S(2)}) %collective-permute-start.1) | collective-permute-done | bytes 153632 | tf_op jit(solution)/shard_map/ppermute | solution.py:599
  25.5 6.3 %collective-permute-done.5.refs_8_.refs_15_ = bf16[4,120,160]{2,1,0:T(8,128)(2,1)S(1)} collective-permute-done((bf16[4,120,160]{2,1,0:T(8,128)(2,1)S(1)}, bf16[4,120,160]{2,1,0:T(8,128)(2,1)S(1)}, u32[]{:S(2)}, u32[]{:S(2)}) %collective-permute-start.5) | collective-permute-done | bytes 153632 | tf_op jit(solution)/shard_map/ppermute | solution.py:594
  38.5 4.1 %all-to-all-start = ((bf16[8,3,80,120]{3,2,1,0:T(8,128)(2,1)}), bf16[8,3,80,120]{3,2,1,0:T(8,128)(2,1)}, u32[]{:S(2)}, u32[]{:S(2)}) async-start(bf16[8,3,80,120]{3,2,1,0:T(8,128)(2,1)} %shard_map.209), calls=%async_computation | async-start | bytes 983040 | tf_op jit(solution)/shard_map/all_to_all | solution.py:727
  61.2 7.5 %collective-permute-done.29.refs_11_ = bf16[128,960]{1,0:T(8,128)(2,1)S(1)} collective-permute-done((bf16[128,960]{1,0:T(8,128)(2,1)}, bf16[128,960]{1,0:T(8,128)(2,1)S(1)}, u32[]{:S(2)}, u32[]{:S(2)}) %collective-permute-start.29) | collective-permute-done | bytes 245792 | tf_op jit(solution)/shard_map/ppermute | solution.py:594
  68.7 4.9 %collective-permute-start.19 = (bf16[136,640]{1,0:T(8,128)(2,1)S(1)}, bf16[136,640]{1,0:T(8,128)(2,1)}, u32[]{:S(2)}, u32[]{:S(2)}) collective-permute-start(bf16[136,640]{1,0:T(8,128)(2,1)S(1)} %get-tuple-element.106.refs_1_.refs_20_), channel_id=1, source_target_pairs={{0,3},{4,7},{8,11},{12,15},{16,19},{20,23},{24,27},{28,31}} | collective-permute-start | bytes 522248 | tf_op jit(solution)/shard_map/ppermute | solution.py:605
  80.6 4.6 %collective-permute-start.34 = (bf16[240,960]{1,0:T(8,128)(2,1)S(1)}, bf16[240,960]{1,0:T(8,128)(2,1)S(1)}, u32[]{:S(2)}, u32[]{:S(2)}) collective-permute-start(bf16[240,960]{1,0:T(8,128)(2,1)S(1)} %shard_map.210.refs_16_), channel_id=1, source_target_pairs={{0,1},{1,2},{2,3},{4,5},{5,6},{6,7},{8,9},{9,10},{10,11},{12,13},{... | collective-permute-start | bytes 1382408 | tf_op jit(solution)/shard_map/ppermute | solution.py:658
  85.9 6.9 %collective-permute-done.37.refs_20_ = bf16[240,960]{1,0:T(8,128)(2,1)S(1)} collective-permute-done((bf16[240,960]{1,0:T(8,128)(2,1)S(1)}, bf16[240,960]{1,0:T(8,128)(2,1)S(1)}, u32[]{:S(2)}, u32[]{:S(2)}) %collective-permute-start.37) | collective-permute-done | bytes 460832 | tf_op jit(solution)/shard_map/ppermute | solution.py:658
  99.9 6.0 %shard_map.207 = (f32[5,384,512]{2,1,0:T(8,128)S(1)}, bf16[128,960]{1,0:T(8,128)(2,1)S(1)}, f32[128,960]{1,0:T(8,128)S(1)}, bf16[128,960]{1,0:T(8,128)(2,1)S(1)}) custom-call(bf16[128,960]{1,0:T(8,128)(2,1)S(1)} %shard_map.206.refs_0_.refs_8_, bf16[136,640]{1,0:T(8,128)(2,1)S(1)} %get-tuple-element.106.refs_1_.refs_20_, ...), custom_call_target="tpu_custom_call" | custom-call | flops 487587840 | bytes 10039552 | tf_op jit(solution)/shard_map/pallas_call | solution.py:575
  117.7 5.0 %collective-permute-done.21.refs_2_ = bf16[128,960]{1,0:T(8,128)(2,1)S(1)} collective-permute-done((bf16[128,960]{1,0:T(8,128)(2,1)S(1)}, bf16[128,960]{1,0:T(8,128)(2,1)S(1)}, u32[]{:S(2)}, u32[]{:S(2)}) %collective-permute-start.21) | collective-permute-done | bytes 245792 | tf_op jit(solution)/shard_map/ppermute | solution.py:594
  124.6 6.2 %collective-permute-done.39.refs_22_ = bf16[240,960]{1,0:T(8,128)(2,1)S(1)} collective-permute-done((bf16[240,960]{1,0:T(8,128)(2,1)S(1)}, bf16[240,960]{1,0:T(8,128)(2,1)S(1)}, u32[]{:S(2)}, u32[]{:S(2)}) %collective-permute-start.39) | collective-permute-done | bytes 460832 | tf_op jit(solution)/shard_map/ppermute | solution.py:658
  130.8 9.5 %shard_map.211 = (bf16[512,960]{1,0:T(8,128)(2,1)S(1)}, bf16[128,960]{1,0:T(8,128)(2,1)S(1)}, bf16[128,960]{1,0:T(8,128)(2,1)S(1)}, bf16[128,960]{1,0:T(8,128)(2...) custom-call(bf16[128,960]{1,0:T(8,128)(2,1)S(1)} %get-tuple-element., ...), custom_call_target="tpu_custom_call" | custom-call | flops 3145728000 | bytes 11089920 | tf_op jit(solution)/shard_map/pallas_call | solution.py:575
  141.4 6.1 %shard_map.212 = (bf16[512,960]{1,0:T(8,128)(2,1)S(1)}, bf16[128,960]{1,0:T(8,128)(2,1)S(1)}, bf16[128,960]{1,0:T(8,128)(2,1)S(1)}, bf16[128,960]{1,0:T(8,128)(2...) custom-call(bf16[128,960]{1,0:T(8,128)(2,1)S(1)} %get-tuple-element., ...), custom_call_target="tpu_custom_call" | custom-call | flops 2516582400 | bytes 14776320 | tf_op jit(solution)/shard_map/pallas_call | solution.py:575
  155.4 6.9 %collective-permute-done.78.refs_2_ = bf16[240,960]{1,0:T(8,128)(2,1)S(1)} collective-permute-done((bf16[240,960]{1,0:T(8,128)(2,1)S(1)}, bf16[240,960]{1,0:T(8,128)(2,1)S(1)}, u32[]{:S(2)}, u32[]{:S(2)}) %collective-permute-start.78) | collective-permute-done | bytes 460832 | tf_op jit(solution)/shard_map/ppermute | solution.py:652
  166.9 6.2 %shard_map.216 = (f32[128,960]{1,0:T(8,128)S(1)}, f32[1,960]{1,0:T(1,128)S(1)}, bf16[128,960]{1,0:T(8,128)(2,1)S(1)}, bf16[128,960]{1,0:T(8,128)(2,1)S(1)}, f32[...) custom-call(f32[128,960]{1,0:T(8,128)S(1)} %get-tuple-element.126.re, ...), custom_call_target="tpu_custom_call" | custom-call | flops 739246080 | bytes 12860928 | tf_op jit(solution)/shard_map/pallas_call | solution.py:575
  177.0 4.0 %collective-permute-start.80 = (bf16[240,960]{1,0:T(8,128)(2,1)S(1)}, bf16[240,960]{1,0:T(8,128)(2,1)S(1)}, u32[]{:S(2)}, u32[]{:S(2)}) collective-permute-start(bf16[240,960]{1,0:T(8,128)(2,1)S(1)} %get-tuple-element.188), channel_id=1, source_target_pairs={{0,1},{1,2},{4,5},{5,6},{8,9},{9,10},{12,13},{13,14},{16,17},{17,1... | collective-permute-start | bytes 1382408 | tf_op jit(solution)/shard_map/ppermute | solution.py:652
  184.4 8.4 %collective-permute-done.55.refs_2_ = bf16[128,640]{1,0:T(8,128)(2,1)S(1)} collective-permute-done((bf16[128,640]{1,0:T(8,128)(2,1)S(1)}, bf16[128,640]{1,0:T(8,128)(2,1)S(1)}, u32[]{:S(2)}, u32[]{:S(2)}) %collective-permute-start.55) | collective-permute-done | bytes 163872 | tf_op jit(solution)/shard_map/ppermute | solution.py:605
  196.9 4.6 %collective-permute-start.82 = (bf16[240,960]{1,0:T(8,128)(2,1)S(1)}, bf16[240,960]{1,0:T(8,128)(2,1)S(1)}, u32[]{:S(2)}, u32[]{:S(2)}) collective-permute-start(bf16[240,960]{1,0:T(8,128)(2,1)S(1)} %get-tuple-element.191), channel_id=1, source_target_pairs={{0,1},{1,2},{2,3},{4,5},{5,6},{6,7},{8,9},{9,10},{10,11},{12,13},{... | collective-permute-start | bytes 1382408 | tf_op jit(solution)/shard_map/ppermute | solution.py:652
  214.4 3.9 %all-to-all-start.1 = ((bf16[8,240,120]{2,1,0:T(8,128)(2,1)}), bf16[8,240,120]{2,1,0:T(8,128)(2,1)S(1)}, u32[]{:S(2)}, u32[]{:S(2)}) async-start(bf16[8,240,120]{2,1,0:T(8,128)(2,1)} %shard_map.227), calls=%async_computation.1 | async-start | bytes 983040 | tf_op jit(solution)/shard_map/all_to_all | solution.py:876
  230.4 5.8 %collective-permute-done.72.refs_1_ = bf16[4,2,120,240]{3,2,1,0:T(8,128)(2,1)} collective-permute-done((bf16[4,2,120,240]{3,2,1,0:T(8,128)(2,1)}, bf16[4,2,120,240]{3,2,1,0:T(8,128)(2,1)}, u32[]{:S(2)}, u32[]{:S(2)}) %collective-permute-start.72) | collective-permute-done | bytes 460832 | tf_op jit(solution)/shard_map/ppermute | solution.py:594
  236.2 4.1 %collective-permute-start.63 = (bf16[496,160]{1,0:T(8,128)(2,1)S(1)}, bf16[496,160]{1,0:T(8,128)(2,1)S(1)}, u32[]{:S(2)}, u32[]{:S(2)}) collective-permute-start(bf16[496,160]{1,0:T(8,128)(2,1)S(1)} %get-tuple-element.153), channel_id=1, source_target_pairs={{0,24},{4,28},{8,16},{12,20},{16,8},{20,12},{24,0},{28,4},{1,25},{... | collective-permute-start | bytes 476168 | tf_op jit(solution)/shard_map/ppermute | solution.py:594
  241.8 7.3 %collective-permute-done.61.refs_0_ = bf16[496,160]{1,0:T(8,128)(2,1)S(1)} collective-permute-done((bf16[496,160]{1,0:T(8,128)(2,1)S(1)}, bf16[496,160]{1,0:T(8,128)(2,1)S(1)}, u32[]{:S(2)}, u32[]{:S(2)}) %collective-permute-start.61) | collective-permute-done | bytes 158752 | tf_op jit(solution)/shard_map/ppermute | solution.py:594
  249.0 11.5 %collective-permute-done.62.refs_1_ = bf16[496,160]{1,0:T(8,128)(2,1)S(1)} collective-permute-done((bf16[496,160]{1,0:T(8,128)(2,1)S(1)}, bf16[496,160]{1,0:T(8,128)(2,1)S(1)}, u32[]{:S(2)}, u32[]{:S(2)}) %collective-permute-start.62) | collective-permute-done | bytes 158752 | tf_op jit(solution)/shard_map/ppermute | solution.py:594
  271.4 6.5 %collective-permute-done.65.refs_1_ = bf16[136,160]{1,0:T(8,128)(2,1)S(1)} collective-permute-done((bf16[136,160]{1,0:T(8,128)(2,1)S(1)}, bf16[136,160]{1,0:T(8,128)(2,1)S(1)}, u32[]{:S(2)}, u32[]{:S(2)}) %collective-permute-start.65) | collective-permute-done | bytes 43552 | tf_op jit(solution)/shard_map/ppermute | solution.py:599
  (273 shorter events, 130.2 us)
Async XLA Ops:
  10.0 32.7 %collective-permute-start.30 = (bf16[128,960]{1,0:T(8,128)(2,1)}, bf16[128,960]{1,0:T(8,128)(2,1)}, u32[]{:S(2)}, u32[]{:S(2)}) collective-permute-start(bf16[128,960]{1,0:T(8,128)(2,1)} %shard_map.208.refs_8_), channel_id=1, source_target_pairs={{0,4},{4,0},{8,12},{12,8},{16,20},{20,16},{24,28},{28,24},{1,5},{5... | collective-permute-start | bytes 737288 | tf_op jit(solution)/shard_map/ppermute | solution.py:594
  25.5 17.6 %collective-permute-start.6 = (bf16[4,120,160]{2,1,0:T(8,128)(2,1)S(1)}, bf16[4,120,160]{2,1,0:T(8,128)(2,1)S(1)}, u32[]{:S(2)}, u32[]{:S(2)}) collective-permute-start(bf16[4,120,160]{2,1,0:T(8,128)(2,1)S(1)} %get-tuple-element.103.refs_5_.refs_12_), channel_id=1, source_target_pairs={{0,4},{4,0},{8,12},{12,8},{16,20},{20,16},{24,28},{28,24},{1,5},{5... | collective-permute-start | bytes 460808 | tf_op jit(solution)/shard_map/ppermute | solution.py:594
  38.5 39.5 %all-to-all-start = ((bf16[8,3,80,120]{3,2,1,0:T(8,128)(2,1)}), bf16[8,3,80,120]{3,2,1,0:T(8,128)(2,1)}, u32[]{:S(2)}, u32[]{:S(2)}) async-start(bf16[8,3,80,120]{3,2,1,0:T(8,128)(2,1)} %shard_map.209), calls=%async_computation | async-start | bytes 983040 | tf_op jit(solution)/shard_map/all_to_all | solution.py:727
  42.7 30.8 %collective-permute-start.13 = (bf16[4,2,120,240]{3,2,1,0:T(8,128)(2,1)S(1)}, bf16[4,2,120,240]{3,2,1,0:T(8,128)(2,1)S(1)}, u32[]{:S(2)}, u32[]{:S(2)}) collective-permute-start(bf16[4,2,120,240]{3,2,1,0:T(8,128)(2,1)S(1)} %get-tuple-element.105.refs_3_.refs_8_.refs_12_.refs_4_), channel_id=1, source_target_pairs={{0,4},{4,0},{8,12},{12,8},{16,20},{20,16},{24,28},{28,24},{1,5},{5... | collective-permute-start | bytes 1382408 | tf_op jit(solution)/shard_map/ppermute | solution.py:594
  43.8 31.7 %collective-permute-start.12 = (bf16[4,2,120,240]{3,2,1,0:T(8,128)(2,1)S(1)}, bf16[4,2,120,240]{3,2,1,0:T(8,128)(2,1)S(1)}, u32[]{:S(2)}, u32[]{:S(2)}) collective-permute-start(bf16[4,2,120,240]{3,2,1,0:T(8,128)(2,1)S(1)} %get-tuple-element.105.refs_3_.refs_8_.refs_12_.refs_4_), channel_id=1, source_target_pairs={{0,24},{4,28},{8,16},{12,20},{16,8},{20,12},{24,0},{28,4},{1,25},{... | collective-permute-start | bytes 1382408 | tf_op jit(solution)/shard_map/ppermute | solution.py:594
  47.1 21.6 %collective-permute-start.29 = (bf16[128,960]{1,0:T(8,128)(2,1)}, bf16[128,960]{1,0:T(8,128)(2,1)S(1)}, u32[]{:S(2)}, u32[]{:S(2)}) collective-permute-start(bf16[128,960]{1,0:T(8,128)(2,1)} %shard_map.208.refs_8_), channel_id=1, source_target_pairs={{0,24},{4,28},{8,16},{12,20},{16,8},{20,12},{24,0},{28,4},{1,25},{... | collective-permute-start | bytes 737288 | tf_op jit(solution)/shard_map/ppermute | solution.py:594
  47.5 31.9 %collective-permute-start.11 = (bf16[4,2,120,240]{3,2,1,0:T(8,128)(2,1)S(1)}, bf16[4,2,120,240]{3,2,1,0:T(8,128)(2,1)S(1)}, u32[]{:S(2)}, u32[]{:S(2)}) collective-permute-start(bf16[4,2,120,240]{3,2,1,0:T(8,128)(2,1)S(1)} %get-tuple-element.105.refs_3_.refs_8_.refs_12_.refs_4_), channel_id=1, source_target_pairs={{0,16},{4,20},{8,24},{12,28},{16,0},{20,4},{24,8},{28,12},{1,17},{... | collective-permute-start | bytes 1382408 | tf_op jit(solution)/shard_map/ppermute | solution.py:594
  49.2 31.4 %collective-permute-start.10 = (bf16[4,2,120,240]{3,2,1,0:T(8,128)(2,1)S(1)}, bf16[4,2,120,240]{3,2,1,0:T(8,128)(2,1)S(1)}, u32[]{:S(2)}, u32[]{:S(2)}) collective-permute-start(bf16[4,2,120,240]{3,2,1,0:T(8,128)(2,1)S(1)} %get-tuple-element.105.refs_3_.refs_8_.refs_12_.refs_4_), channel_id=1, source_target_pairs={{0,8},{4,12},{8,0},{12,4},{16,24},{20,28},{24,16},{28,20},{1,9},{5... | collective-permute-start | bytes 1382408 | tf_op jit(solution)/shard_map/ppermute | solution.py:594
  95.5 17.7 %collective-permute-start.38 = (bf16[240,960]{1,0:T(8,128)(2,1)S(1)}, bf16[240,960]{1,0:T(8,128)(2,1)S(1)}, u32[]{:S(2)}, u32[]{:S(2)}) collective-permute-start(bf16[240,960]{1,0:T(8,128)(2,1)S(1)} %collective-permute-done.37.refs_20_), channel_id=1, source_target_pairs={{1,0},{2,1},{5,4},{6,5},{9,8},{10,9},{13,12},{14,13},{17,16},{18,1... | collective-permute-start | bytes 1382408 | tf_op jit(solution)/shard_map/ppermute | solution.py:658
  96.8 17.7 %collective-permute-start.35 = (bf16[240,960]{1,0:T(8,128)(2,1)S(1)}, bf16[240,960]{1,0:T(8,128)(2,1)S(1)}, u32[]{:S(2)}, u32[]{:S(2)}) collective-permute-start(bf16[240,960]{1,0:T(8,128)(2,1)S(1)} %collective-permute-done.34.refs_17_), channel_id=1, source_target_pairs={{1,2},{2,3},{5,6},{6,7},{9,10},{10,11},{13,14},{14,15},{17,18},{18... | collective-permute-start | bytes 1382408 | tf_op jit(solution)/shard_map/ppermute | solution.py:658
  155.4 17.7 %collective-permute-start.40 = (bf16[128,960]{1,0:T(8,128)(2,1)S(1)}, bf16[128,960]{1,0:T(8,128)(2,1)S(1)}, u32[]{:S(2)}, u32[]{:S(2)}) collective-permute-start(bf16[128,960]{1,0:T(8,128)(2,1)S(1)} %get-tuple-element.113), channel_id=1, source_target_pairs={{0,4},{4,0},{8,12},{12,8},{16,20},{20,16},{24,28},{28,24},{1,5},{5... | collective-permute-start | bytes 737288 | tf_op jit(solution)/shard_map/ppermute | solution.py:594
  162.5 30.8 %collective-permute-start.79 = (bf16[240,960]{1,0:T(8,128)(2,1)S(1)}, bf16[240,960]{1,0:T(8,128)(2,1)S(1)}, u32[]{:S(2)}, u32[]{:S(2)}) collective-permute-start(bf16[240,960]{1,0:T(8,128)(2,1)S(1)} %get-tuple-element.186), channel_id=1, source_target_pairs={{2,1},{3,2},{6,5},{7,6},{10,9},{11,10},{14,13},{15,14},{18,17},{19... | collective-permute-start | bytes 1382408 | tf_op jit(solution)/shard_map/ppermute | solution.py:652
  174.4 18.4 %collective-permute-start.55 = (bf16[128,640]{1,0:T(8,128)(2,1)S(1)}, bf16[128,640]{1,0:T(8,128)(2,1)S(1)}, u32[]{:S(2)}, u32[]{:S(2)}) collective-permute-start(bf16[128,640]{1,0:T(8,128)(2,1)S(1)} %get-tuple-element.134), channel_id=1, source_target_pairs={{2,0},{3,1},{6,4},{7,5},{10,8},{11,9},{14,12},{15,13},{18,16},{19,... | collective-permute-start | bytes 491528 | tf_op jit(solution)/shard_map/ppermute | solution.py:605
  207.8 22.1 %collective-permute-start.71 = (bf16[4,2,120,240]{3,2,1,0:T(8,128)(2,1)}, bf16[4,2,120,240]{3,2,1,0:T(8,128)(2,1)}, u32[]{:S(2)}, u32[]{:S(2)}) collective-permute-start(bf16[4,2,120,240]{3,2,1,0:T(8,128)(2,1)} %get-tuple-element.169), channel_id=1, source_target_pairs={{0,8},{4,12},{8,0},{12,4},{16,24},{20,28},{24,16},{28,20},{1,9},{5... | collective-permute-start | bytes 1382408 | tf_op jit(solution)/shard_map/ppermute | solution.py:594
  209.5 26.6 %collective-permute-start.72 = (bf16[4,2,120,240]{3,2,1,0:T(8,128)(2,1)}, bf16[4,2,120,240]{3,2,1,0:T(8,128)(2,1)}, u32[]{:S(2)}, u32[]{:S(2)}) collective-permute-start(bf16[4,2,120,240]{3,2,1,0:T(8,128)(2,1)} %get-tuple-element.170), channel_id=1, source_target_pairs={{0,16},{4,20},{8,24},{12,28},{16,0},{20,4},{24,8},{28,12},{1,17},{... | collective-permute-start | bytes 1382408 | tf_op jit(solution)/shard_map/ppermute | solution.py:594
  211.0 25.2 %collective-permute-start.73 = (bf16[4,2,120,240]{3,2,1,0:T(8,128)(2,1)}, bf16[4,2,120,240]{3,2,1,0:T(8,128)(2,1)}, u32[]{:S(2)}, u32[]{:S(2)}) collective-permute-start(bf16[4,2,120,240]{3,2,1,0:T(8,128)(2,1)} %get-tuple-element.171), channel_id=1, source_target_pairs={{0,24},{4,28},{8,16},{12,20},{16,8},{20,12},{24,0},{28,4},{1,25},{... | collective-permute-start | bytes 1382408 | tf_op jit(solution)/shard_map/ppermute | solution.py:594
  214.4 65.0 %all-to-all-start.1 = ((bf16[8,240,120]{2,1,0:T(8,128)(2,1)}), bf16[8,240,120]{2,1,0:T(8,128)(2,1)S(1)}, u32[]{:S(2)}, u32[]{:S(2)}) async-start(bf16[8,240,120]{2,1,0:T(8,128)(2,1)} %shard_map.227), calls=%async_computation.1 | async-start | bytes 983040 | tf_op jit(solution)/shard_map/all_to_all | solution.py:876
  219.0 44.0 %collective-permute-start.45 = (bf16[128,960]{1,0:T(8,128)(2,1)}, bf16[128,960]{1,0:T(8,128)(2,1)S(1)}, u32[]{:S(2)}, u32[]{:S(2)}) collective-permute-start(bf16[128,960]{1,0:T(8,128)(2,1)} %copy-done.48), channel_id=1, source_target_pairs={{0,16},{4,20},{8,24},{12,28},{16,0},{20,4},{24,8},{28,12},{1,17},{... | collective-permute-start | bytes 737288 | tf_op jit(solution)/shard_map/ppermute | solution.py:594
  220.7 43.6 %collective-permute-start.46 = (bf16[128,960]{1,0:T(8,128)(2,1)}, bf16[128,960]{1,0:T(8,128)(2,1)S(1)}, u32[]{:S(2)}, u32[]{:S(2)}) collective-permute-start(bf16[128,960]{1,0:T(8,128)(2,1)} %copy-done.47), channel_id=1, source_target_pairs={{0,24},{4,28},{8,16},{12,20},{16,8},{20,12},{24,0},{28,4},{1,25},{... | collective-permute-start | bytes 737288 | tf_op jit(solution)/shard_map/ppermute | solution.py:594
  229.9 19.1 %collective-permute-start.61 = (bf16[496,160]{1,0:T(8,128)(2,1)S(1)}, bf16[496,160]{1,0:T(8,128)(2,1)S(1)}, u32[]{:S(2)}, u32[]{:S(2)}) collective-permute-start(bf16[496,160]{1,0:T(8,128)(2,1)S(1)} %get-tuple-element.151), channel_id=1, source_target_pairs={{0,8},{4,12},{8,0},{12,4},{16,24},{20,28},{24,16},{28,20},{1,9},{5... | collective-permute-start | bytes 476168 | tf_op jit(solution)/shard_map/ppermute | solution.py:594
  236.1 24.4 %collective-permute-start.62 = (bf16[496,160]{1,0:T(8,128)(2,1)S(1)}, bf16[496,160]{1,0:T(8,128)(2,1)S(1)}, u32[]{:S(2)}, u32[]{:S(2)}) collective-permute-start(bf16[496,160]{1,0:T(8,128)(2,1)S(1)} %get-tuple-element.152), channel_id=1, source_target_pairs={{0,16},{4,20},{8,24},{12,28},{16,0},{20,4},{24,8},{28,12},{1,17},{... | collective-permute-start | bytes 476168 | tf_op jit(solution)/shard_map/ppermute | solution.py:594
  236.2 24.9 %collective-permute-start.63 = (bf16[496,160]{1,0:T(8,128)(2,1)S(1)}, bf16[496,160]{1,0:T(8,128)(2,1)S(1)}, u32[]{:S(2)}, u32[]{:S(2)}) collective-permute-start(bf16[496,160]{1,0:T(8,128)(2,1)S(1)} %get-tuple-element.153), channel_id=1, source_target_pairs={{0,24},{4,28},{8,16},{12,20},{16,8},{20,12},{24,0},{28,4},{1,25},{... | collective-permute-start | bytes 476168 | tf_op jit(solution)/shard_map/ppermute | solution.py:594
  249.0 29.6 %collective-permute-start.74 = (bf16[2,120,240]{2,1,0:T(8,128)(2,1)S(1)}, bf16[2,120,240]{2,1,0:T(8,128)(2,1)S(1)}, u32[]{:S(2)}, u32[]{:S(2)}) collective-permute-start(bf16[2,120,240]{2,1,0:T(8,128)(2,1)S(1)} %get-tuple-element.173), channel_id=1, source_target_pairs={{0,1},{1,0},{2,3},{3,2},{4,5},{5,4},{6,7},{7,6},{8,9},{9,8},{10,11... | collective-permute-start | bytes 345608 | tf_op jit(solution)/shard_map/ppermute | solution.py:599
  260.5 18.1 %collective-permute-start.75 = (bf16[2,120,240]{2,1,0:T(8,128)(2,1)S(1)}, bf16[2,120,240]{2,1,0:T(8,128)(2,1)S(1)}, u32[]{:S(2)}, u32[]{:S(2)}) collective-permute-start(bf16[2,120,240]{2,1,0:T(8,128)(2,1)S(1)} %get-tuple-element.174), channel_id=1, source_target_pairs={{0,2},{1,3},{2,0},{3,1},{4,6},{5,7},{6,4},{7,5},{8,10},{9,11},{10,... | collective-permute-start | bytes 345608 | tf_op jit(solution)/shard_map/ppermute | solution.py:599
  (110 other events, 1328.0 us)
